TPU v7x, 32 devices: a whole 2x2x4 slice. The times are simulated.
32 devices in a mesh: batch: 4 (over y, core), wide: 8 (over z, x).
Axes of the slice: x: 2, y: 2, z: 4, core: 2. Of those that a mesh axis runs over, the one named last changes fastest.
Arguments:
- inputs: bfloat16 [32, 512, 768], P(('batch', 'wide')), may hold values from -6 to 6
- lengths: int32 [32], P(('batch', 'wide')), may hold values from 1 to 512, 6553 in all
- cotangent: bfloat16 [32, 512, 768], P(('batch', 'wide')), may hold values from -6 to 6
- w_qkv: bfloat16 [768, 2304], P(('batch', 'wide')), may hold values from -0.21875 to 0.21875
- w_out: bfloat16 [768, 768], P(('batch', 'wide')), may hold values from -3.5 to 3.5
- conv_taps: bfloat16 [2304, 3], P(('batch', 'wide')), may hold values from -3.5 to 3.5
- gain_one: bfloat16 [768], P(('batch', 'wide')), may hold values from 0.099609375 to 1.8984375
- gain_two: bfloat16 [768], P(('batch', 'wide')), may hold values from 0.099609375 to 1.8984375
- w_in: bfloat16 [768, 3072], P(None, 'wide'), may hold values from -0.21875 to 0.21875
- w_fc2: bfloat16 [3072, 768], P('wide'), may hold values from -0.109375 to 0.109375
Outputs:
- output: bfloat16 [32, 512, 768], P(('batch', 'wide'))
- grad_inputs: bfloat16 [32, 512, 768], P(('batch', 'wide'))
- grad_w_qkv: float32 [768, 2304], P(('batch', 'wide'))
- grad_w_out: float32 [768, 768], P(('batch', 'wide'))
- grad_conv_taps: float32 [2304, 3], P(('batch', 'wide'))
- grad_gain_one: float32 [768], P(('batch', 'wide'))
- grad_gain_two: float32 [768], P(('batch', 'wide'))
- grad_w_in: float32 [768, 3072], P('batch', 'wide')
- grad_w_fc2: float32 [3072, 768], P('wide', 'batch')
Inputs may be any that keep to these rules, and one draw needn't show every extreme that they name: lengths[s] is the number of real tokens of sequence s; the longest has exactly 512.
All inputs are finite; a program needn't handle non-finite values. No bound on the sum of `lengths` on one device may be relied on, other than what follows from the above.
Results may differ from a plain program's by a relative error of at most 0.017.
Values may be sent and summed in bfloat16 or wider, within the bound.
No kernel may reach another device: no remote copies, remote signals or barrier semaphores. Data moves between devices by JAX's collectives and lax.ppermute only.
A program may use at most 256 MiB of HBM per device.

v0:
```python
import jax
import jax.numpy as jnp
from jax import lax
from jax.sharding import PartitionSpec as P

HEADS = 12
HD = 64


epsilon = 1e-05


def contract_first(left, right):
    return lax.dot_general(
        left, right, (((0,), (0,)), ((), ())), preferred_element_type=jnp.float32
    )


def contract_last(left, right):
    return lax.dot_general(
        left, right, (((1,), (1,)), ((), ())), preferred_element_type=jnp.float32
    )


def norm_parts(values_in):
    centered = values_in - jnp.mean(values_in, axis=-1, keepdims=True)
    inv_std = lax.rsqrt(jnp.mean(centered * centered, axis=-1, keepdims=True) + epsilon)
    return (centered * inv_std, inv_std)


def norm_back(grad_normed, gain_vec, normed_hat, inv_std):
    grad_hat = grad_normed * gain_vec
    mean_first = jnp.mean(grad_hat, axis=-1, keepdims=True)
    mean_second = jnp.mean(grad_hat * normed_hat, axis=-1, keepdims=True)
    grad_value = inv_std * (grad_hat - mean_first - normed_hat * mean_second)
    return (grad_value, jnp.sum(grad_normed * normed_hat, axis=0))


def shift_down(signal, steps):
    filler = jnp.zeros((steps, signal.shape[1]), signal.dtype)
    return jnp.concatenate([filler, signal[:-steps]], axis=0)


def shift_up(signal, steps):
    filler = jnp.zeros((steps, signal.shape[1]), signal.dtype)
    return jnp.concatenate([signal[steps:], filler], axis=0)


def scores_block(query_block, keys, start_row, seq_live):
    rows_block = query_block.shape[0]
    scores = (
        jnp.einsum("qhd,khd->hqk", query_block, keys, preferred_element_type=jnp.float32) * 0.125
    )
    query_pos = start_row + jnp.arange(rows_block)
    key_pos = jnp.arange(keys.shape[0])
    allowed = (key_pos[None, :] <= query_pos[:, None]) & (key_pos[None, :] < seq_live)
    return (scores, allowed[None])


def shards(inputs, lengths, cotangent, w_qkv, w_out, conv_taps, gain_one, gain_two, w_in, w_fc2):
    full_qkv, full_out, full_taps, full_gain_one, full_gain_two = (
        lax.all_gather(w_qkv, ("batch", "wide"), axis=0, tiled=True),
        lax.all_gather(w_out, ("batch", "wide"), axis=0, tiled=True),
        lax.all_gather(conv_taps, ("batch", "wide"), axis=0, tiled=True),
        lax.all_gather(gain_one, ("batch", "wide"), axis=0, tiled=True),
        lax.all_gather(gain_two, ("batch", "wide"), axis=0, tiled=True),
    )
    seq_length, width = (inputs.shape[1], inputs.shape[2])
    tokens_in = inputs[0].astype(jnp.float32)
    seq_live = lengths[0]
    live_rows = jnp.arange(seq_length) < seq_live
    taps = full_taps.astype(jnp.float32)
    gain_first = full_gain_one.astype(jnp.float32)
    gain_second = full_gain_two.astype(jnp.float32)
    hat_one, inv_one = norm_parts(tokens_in)
    normed_one = (hat_one * gain_first).astype(jnp.bfloat16)
    projected = jnp.dot(normed_one, full_qkv, preferred_element_type=jnp.float32)
    mixed = (
        projected * taps[:, 0]
        + shift_down(projected, 1) * taps[:, 1]
        + shift_down(projected, 2) * taps[:, 2]
    ).astype(jnp.bfloat16)
    query = mixed[:, :width].reshape(seq_length, HEADS, HD)
    keys = mixed[:, width : 2 * width].reshape(seq_length, HEADS, HD)
    values = mixed[:, 2 * width :].reshape(seq_length, HEADS, HD)
    rows_block = min(512, seq_length)
    block_index = 0
    start_row = block_index * rows_block
    scores, allowed = scores_block(query, keys, start_row, seq_live)
    masked = jnp.where(allowed, scores, -1e30)
    top_score = jnp.max(masked, axis=-1, keepdims=True)
    exp_terms = jnp.exp(masked - top_score)
    row_totals = jnp.sum(exp_terms, axis=-1, keepdims=True)
    probs_low = (exp_terms / row_totals).astype(jnp.bfloat16)
    out_parts = jnp.einsum("hqk,khd->qhd", probs_low, values, preferred_element_type=jnp.float32)
    lse_parts = [top_score + jnp.log(row_totals)]
    attended_low = out_parts.reshape(seq_length, width).astype(jnp.bfloat16)
    branch_attn = jnp.dot(attended_low, full_out, preferred_element_type=jnp.float32)
    residual = tokens_in + branch_attn
    hat_two, inv_two = norm_parts(residual)
    normed_two = (hat_two * gain_second).astype(jnp.bfloat16)
    grad_out = jnp.where(live_rows[:, None], cotangent[0], jnp.zeros_like(cotangent[0]))
    row_set = lax.all_gather(normed_two[None], "wide", axis=0, tiled=True).reshape(-1, width)
    pre_act = jnp.dot(row_set, w_in, preferred_element_type=jnp.float32)
    activ = jnp.square(jax.nn.relu(pre_act)).astype(jnp.bfloat16)
    piece = activ
    branch_ffn = lax.psum_scatter(
        jnp.dot(piece, w_fc2, preferred_element_type=jnp.float32).astype(jnp.bfloat16),
        "wide",
        scatter_dimension=0,
        tiled=True,
    ).astype(jnp.float32)
    grad_set = lax.all_gather(grad_out[None], "wide", axis=0, tiled=True).reshape(-1, width)
    grad_act = contract_last(grad_set, w_fc2)
    grad_fc2_part = contract_first(activ, grad_set)
    grad_pre = (grad_act * 2.0 * jax.nn.relu(pre_act)).astype(jnp.bfloat16)
    grad_in_part = contract_first(row_set, grad_pre)
    piece = grad_pre
    grad_normed_two = lax.psum_scatter(
        contract_last(piece, w_in).astype(jnp.bfloat16), "wide", scatter_dimension=0, tiled=True
    ).astype(jnp.float32)
    grad_w_in, grad_w_fc2 = (
        lax.psum_scatter(
            grad_in_part.astype(jnp.bfloat16), "batch", scatter_dimension=0, tiled=True
        ).astype(jnp.float32),
        lax.psum_scatter(
            grad_fc2_part.astype(jnp.bfloat16), "batch", scatter_dimension=1, tiled=True
        ).astype(jnp.float32),
    )
    output = jnp.where(live_rows[:, None], residual + branch_ffn, 0.0).astype(jnp.bfloat16)[None]
    grad_ln_two, grad_gain_second = norm_back(grad_normed_two, gain_second, hat_two, inv_two)
    grad_residual = grad_out.astype(jnp.float32) + grad_ln_two
    grad_branch = grad_residual.astype(jnp.bfloat16)
    grad_w_out_part = contract_first(attended_low, grad_branch)
    grad_attended = contract_last(grad_branch, full_out).astype(jnp.bfloat16)
    grad_att_heads = grad_attended.reshape(seq_length, HEADS, HD)
    delta_all = jnp.sum(grad_att_heads.astype(jnp.float32) * out_parts, axis=-1)
    block_index = 0
    start_row = block_index * rows_block
    scores, allowed = scores_block(query, keys, start_row, seq_live)
    probs_full = jnp.where(allowed, jnp.exp(scores - lse_parts[block_index]), 0.0)
    probs_low = probs_full.astype(jnp.bfloat16)
    grad_probs = jnp.einsum(
        "qhd,khd->hqk", grad_att_heads, values, preferred_element_type=jnp.float32
    )
    delta_block = jnp.transpose(delta_all)[:, :, None]
    grad_scores = (probs_full * (grad_probs - delta_block)).astype(jnp.bfloat16)
    grad_query_parts = 0.125 * jnp.einsum(
        "hqk,khd->qhd", grad_scores, keys, preferred_element_type=jnp.float32
    )
    grad_keys = 0.125 * jnp.einsum(
        "hqk,qhd->khd", grad_scores, query, preferred_element_type=jnp.float32
    )
    grad_values = jnp.einsum(
        "hqk,qhd->khd", probs_low, grad_att_heads, preferred_element_type=jnp.float32
    )
    grad_mixed = jnp.concatenate(
        [
            grad_query_parts.reshape(seq_length, width),
            grad_keys.reshape(seq_length, width),
            grad_values.reshape(seq_length, width),
        ],
        axis=1,
    )
    grad_taps_part = jnp.stack(
        [
            jnp.sum(grad_mixed * projected, axis=0),
            jnp.sum(grad_mixed * shift_down(projected, 1), axis=0),
            jnp.sum(grad_mixed * shift_down(projected, 2), axis=0),
        ],
        axis=1,
    )
    grad_projected = (
        grad_mixed * taps[:, 0]
        + shift_up(grad_mixed, 1) * taps[:, 1]
        + shift_up(grad_mixed, 2) * taps[:, 2]
    ).astype(jnp.bfloat16)
    grad_qkv_part = contract_first(normed_one, grad_projected)
    grad_normed_one = contract_last(grad_projected, full_qkv)
    grad_ln_one, grad_gain_first = norm_back(grad_normed_one, gain_first, hat_one, inv_one)
    grad_inputs = (grad_residual + grad_ln_one).astype(jnp.bfloat16)[None]
    grad_w_qkv, grad_w_out, grad_conv_taps, grad_gain_one, grad_gain_two = (
        lax.psum_scatter(grad_qkv_part, ("batch", "wide"), scatter_dimension=0, tiled=True),
        lax.psum_scatter(grad_w_out_part, ("batch", "wide"), scatter_dimension=0, tiled=True),
        lax.psum_scatter(grad_taps_part, ("batch", "wide"), scatter_dimension=0, tiled=True),
        lax.psum_scatter(grad_gain_first, ("batch", "wide"), scatter_dimension=0, tiled=True),
        lax.psum_scatter(grad_gain_second, ("batch", "wide"), scatter_dimension=0, tiled=True),
    )
    return (
        output,
        grad_inputs,
        grad_w_qkv,
        grad_w_out,
        grad_conv_taps,
        grad_gain_one,
        grad_gain_two,
        grad_w_in,
        grad_w_fc2,
    )


def solution(mesh):
    return jax.shard_map(
        shards,
        mesh=mesh,
        in_specs=(
            P(("batch", "wide"), None, None),
            P(("batch", "wide")),
            P(("batch", "wide"), None, None),
            P(("batch", "wide"), None),
            P(("batch", "wide"), None),
            P(("batch", "wide"), None),
            P(("batch", "wide")),
            P(("batch", "wide")),
            P(None, "wide"),
            P("wide", None),
        ),
        out_specs=(
            P(("batch", "wide"), None, None),
            P(("batch", "wide"), None, None),
            P(("batch", "wide"), None),
            P(("batch", "wide"), None),
            P(("batch", "wide"), None),
            P(("batch", "wide")),
            P(("batch", "wide")),
            P("batch", "wide"),
            P("wide", "batch"),
        ),
        check_vma=False,
    )
```

profile of v0, /device:TPU:0, one launch (start us, length us, event | category | flops | bytes accessed | tf_op | source)
XLA Modules:
  0.0 884.9 jit_solution(11334674842773238938)
XLA Ops:
  7.2 0.7 all-gather.7.cloned.1.call-update
  8.0 0.7 all-gather.9.cloned.1.call-update
  9.4 1.3 convert_reduce_fusion
  10.7 1.5 fusion.24
  12.2 0.8 dynamic-update-slice
  13.1 0.8 dynamic-update-slice.1
  13.9 42.1 %all-reduce.10 = (bf16[768]{0:T(1024)(128)(2,1)S(1)}, bf16[768]{0:T(1024)(128)(2,1)S(1)}) all-reduce(bf16[768]{0:T(1024)(128)(2,1)S(1)} %dynamic-update-slice, bf16[768]{0:T(1024)(128)(2,1)S(1)} %dynamic-update-slice.1), channel_id=1, replica_groups=mesh['batch'=4,'wide'=8] {'batch','wide'}, use_global_device_ids=true, to_apply=%add.4 | all-reduce | flops 1536 | bytes 6144
  56.0 66.4 %all-gather.1 = bf16[32,72,3]{1,2,0:T(4,128)(2,1)S(1)} all-gather(bf16[1,72,3]{1,2,0:T(4,128)(2,1)} %bitcast.127), channel_id=1, replica_groups=mesh['batch'=4,'wide'=8] {'batch','wide'}, dimensions={0}, use_global_device_ids=true | all-gather | bytes 14256 | tf_op jit(solution)/shard_map/all_gather | solution.py:64
  122.8 4.4 fusion.43
  127.2 1.5 add_convert_fusion.1
  128.7 0.7 copy-done.2
  129.4 1.0 fusion.45
  130.7 1.4 copy.62
  132.1 2.1 select_reduce_fusion
  134.2 2.6 fusion
  136.8 2.0 copy-done.3
  138.8 0.3 copy.61
  139.1 8.3 bitcast_convert_fusion
  147.3 2.6 fusion.46
  150.0 0.3 multiply_reduce_fusion.3
  150.3 1.2 multiply_convert_fusion.3
  151.5 2.2 broadcast_select_fusion
  153.8 93.8 %all-gather.13.cloned.1.call-done = bf16[4096,768]{1,0:T(8,128)(2,1)} async-done(((bf16[512,768]{1,0:T(8,128)(2,1)}), bf16[4096,768]{1,0:T(8,128)(2,1)}) %all-gather.13.cloned.1.call-update) | async-done | bytes 6291472 | tf_op jit(solution)/shard_map/all_gather | solution.py:103
  247.6 8.9 %convolution_maximum_fusion = f32[4096,384]{1,0:T(8,128)} fusion(bf16[4096,768]{1,0:T(8,128)(2,1)} %all-gather.13.cloned.1.call-done, bf16[768,384]{1,0:T(8,128)(2,1)S(1)} %copy-done), kind=kOutput, calls=%fused_computation.14 | convolution fusion | flops 2417491968 | bytes 13172736 | tf_op jit(solution)/shard_map/dot_general | solution.py:104
  256.5 90.1 %all-gather.11.cloned.1.call-done = bf16[8,512,768]{2,1,0:T(8,128)(2,1)} async-done(((bf16[1,512,768]{2,1,0:T(8,128)(2,1)}), bf16[8,512,768]{2,1,0:T(8,128)(2,1)}) %all-gather.11.cloned.1.call-update) | async-done | bytes 6291472 | tf_op jit(solution)/shard_map/all_gather | solution.py:113
  346.5 8.2 multiply_convert_fusion.1
  354.8 1.7 copy-done.9
  356.5 5.4 convolution_convert_fusion
  361.9 10.3 %reduce-scatter.8.cloned.1.call-start = ((), (), s32[]{:S(2)}) async-start(), calls=%async_computation.8 | async-start | bytes 7077888 | tf_op jit(solution)/shard_map/reduce_scatter | solution.py:107
  372.2 9.0 %convolution_convert_fusion.1 = bf16[4096,768]{1,0:T(8,128)(2,1)} fusion(bf16[384,768]{1,0:T(8,128)(2,1)S(1)} %copy-done.10, f32[4096,384]{1,0:T(8,128)} %convolution_maximum_fusion), kind=kOutput, calls=%fused_computation.8 | convolution fusion | flops 2422210560 | bytes 13172736 | tf_op jit(solution)/shard_map/dot_general | solution.py:108
  381.3 9.0 %convolution_convert_fusion.3 = bf16[384,768]{0,1:T(8,128)(2,1)} fusion(bf16[4096,768]{1,0:T(8,128)(2,1)} %bitcast.114, f32[4096,384]{1,0:T(8,128)} %convolution_maximum_fusion), kind=kOutput, calls=%fused_computation.60 | convolution fusion | flops 2419359744 | bytes 13172736 | tf_op jit(solution)/shard_map/dot_general | solution.py:14
  390.4 8.3 convolution_convert_fusion.4
  398.8 79.5 %reduce-scatter.10.cloned.1.call-done = bf16[512,768]{1,0:T(8,128)(2,1)} async-done(((bf16[4096,768]{1,0:T(8,128)(2,1)}), bf16[512,768]{1,0:T(8,128)(2,1)}) %reduce-scatter.10.cloned.1.call-update) | async-done | bytes 786448 | tf_op jit(solution)/shard_map/reduce_scatter | solution.py:119
  478.3 1.9 fusion.29
  480.2 118.8 %reduce-scatter.8.cloned.1.call-done = bf16[512,768]{1,0:T(8,128)(2,1)} async-done(((bf16[4096,768]{1,0:T(8,128)(2,1)}), bf16[512,768]{1,0:T(8,128)(2,1)}) %reduce-scatter.8.cloned.1.call-update) | async-done | bytes 786448 | tf_op jit(solution)/shard_map/reduce_scatter | solution.py:107
  599.0 3.0 fusion.27
  602.1 1.2 copy-done.4
  603.3 2.2 fusion.34
  605.4 3.5 convolution_convert_fusion.2
  609.0 1.4 copy.65
  610.4 1.7 fusion.30
  612.1 8.5 multiply_convert_fusion
  620.9 7.2 fusion.2
  628.1 1.9 copy.72
  630.0 5.1 convolution_multiply_fusion.1
  635.1 3.1 copy.70
  638.2 5.9 convolution_multiply_fusion
  644.2 3.0 copy.71
  647.2 2.2 pad_maximum_fusion
  649.4 0.3 slice.53
  649.7 0.3 slice.54
  650.0 1.5 slice-done
  651.8 6.6 multiply_reduce_fusion.2
  658.4 6.8 fusion.41
  665.2 1.6 convert_element_type.119
  666.8 1.6 convert_element_type.117
  668.6 6.3 fusion.23
  674.9 40.7 %all-reduce.9 = (f32[2304,3]{0,1:T(4,128)S(1)}, f32[768]{0:T(1024)S(1)}, f32[768]{0:T(1024)S(1)}) all-reduce(f32[2304,3]{0,1:T(4,128)S(1)} %pad_maximum_fusion.1, f32[768]{0:T(1024)S(1)} %get-tuple-element.14, f32[768]{0:T(1024)S(1)} %get-tuple-element.12), channel_id=7, replica_groups=mesh['batch'=4,'wide'=8] {'batch','wide'}, use_global_device_ids=true, to_apply=%region_18.19.clone | all-reduce | flops 8448 | bytes 67584
  715.6 0.6 dynamic-slice.1
  716.2 0.6 dynamic-slice.2
  716.8 0.6 constant_dynamic-slice_fusion
  717.5 2.8 fusion.33
  720.3 32.6 %reduce-scatter.14.cloned.1.call-done = f32[24,768]{1,0:T(8,128)} async-done(((f32[768,768]{1,0:T(8,128)}), f32[24,768]{1,0:T(8,128)}) %reduce-scatter.14.cloned.1.call-update) | async-done | bytes 73744 | tf_op jit(solution)/shard_map/reduce_scatter | solution.py:184
  752.9 124.7 %reduce-scatter.12.cloned.1.call-done = f32[24,2304]{1,0:T(8,128)} async-done(((f32[768,2304]{1,0:T(8,128)}), f32[24,2304]{1,0:T(8,128)}) %reduce-scatter.12.cloned.1.call-update) | async-done | bytes 221200 | tf_op jit(solution)/shard_map/reduce_scatter | solution.py:183
  (71 shorter events, 1.7 us)
Async XLA Ops:
  7.2 240.4 %copy-start = (bf16[768,384]{1,0:T(8,128)(2,1)S(1)}, bf16[768,384]{1,0:T(8,128)(2,1)}, u32[]{:S(2)}) copy-start(bf16[768,384]{1,0:T(8,128)(2,1)} %param.18) | copy-start | bytes 1769476
  7.2 115.6 %all-gather.7.cloned.1.call-start = ((), (), s32[]{:S(2)}) async-start(), calls=%async_computation.6 | async-start | bytes 3649536 | tf_op jit(solution)/shard_map/all_gather | solution.py:62
  7.9 139.4 %all-gather.9.cloned.1.call-start = ((), (), s32[]{:S(2)}) async-start(), calls=%async_computation.7 | async-start | bytes 1216512 | tf_op jit(solution)/shard_map/all_gather | solution.py:63
  8.7 238.9 %all-gather.13.cloned.1.call-start = ((), (), s32[]{:S(2)}) async-start(), calls=%async_computation.15 | async-start | bytes 7077888 | tf_op jit(solution)/shard_map/all_gather | solution.py:103
  127.2 2.2 copy-start.2
  132.1 2.1 copy-start.6
  134.2 4.6 copy-start.3
  139.1 8.3 copy-start.12
  151.5 195.1 %all-gather.11.cloned.1.call-start = ((), (), s32[]{:S(2)}) async-start(), calls=%async_computation.9 | async-start | bytes 7077888 | tf_op jit(solution)/shard_map/all_gather | solution.py:113
  153.7 324.6 %reduce-scatter.10.cloned.1.call-start = ((), (), s32[]{:S(2)}) async-start(), calls=%async_computation.10 | async-start | bytes 7077888 | tf_op jit(solution)/shard_map/reduce_scatter | solution.py:119
  354.8 1.7 copy-start.9
  361.9 10.3 %copy-start.10 = (bf16[384,768]{1,0:T(8,128)(2,1)S(1)}, bf16[384,768]{1,0:T(8,128)(2,1)}, u32[]{:S(2)}) copy-start(bf16[384,768]{1,0:T(8,128)(2,1)} %param.19) | copy-start | bytes 1769476
  361.9 237.1 %reduce-scatter.8.cloned.1.call-start = ((), (), s32[]{:S(2)}) async-start(), calls=%async_computation.8 | async-start | bytes 7077888 | tf_op jit(solution)/shard_map/reduce_scatter | solution.py:107
  381.2 284.0 %reduce-scatter.18.cloned.1.call-start = ((), (), s32[]{:S(2)}) async-start(), calls=%async_computation.14 | async-start | bytes 737280 | tf_op jit(solution)/shard_map/reduce_scatter | solution.py:126
  390.3 276.5 %reduce-scatter.16.cloned.1.call-start = ((), (), s32[]{:S(2)}) async-start(), calls=%async_computation.13 | async-start | bytes 737280 | tf_op jit(solution)/shard_map/reduce_scatter | solution.py:123
  398.7 354.2 %reduce-scatter.14.cloned.1.call-start = ((), (), s32[]{:S(2)}) async-start(), calls=%async_computation.12 | async-start | bytes 2433024 | tf_op jit(solution)/shard_map/reduce_scatter | solution.py:184
  599.0 4.2 copy-start.11
  602.1 1.2 copy-start.4
  605.4 6.7 copy-start.13
  620.6 257.0 %reduce-scatter.12.cloned.1.call-start = ((), (), s32[]{:S(2)}) async-start(), calls=%async_computation.11 | async-start | bytes 7299072 | tf_op jit(solution)/shard_map/reduce_scatter | solution.py:183
  635.1 3.1 copy-start.7
  649.4 2.2 slice-start
  649.7 2.0 slice-start.1
  651.8 6.6 copy-start.8
  668.6 48.9 %copy-start.5 = (f32[512,768]{1,0:T(8,128)S(1)}, f32[512,768]{1,0:T(8,128)}, u32[]{:S(2)}) copy-start(f32[512,768]{1,0:T(8,128)} %copy-done.4) | copy-start | bytes 4718596
  668.6 209.1 %copy-start.1 = (bf16[768,384]{1,0:T(8,128)(2,1)S(1)}, bf16[768,384]{1,0:T(8,128)(2,1)}, u32[]{:S(2)}) copy-start(bf16[768,384]{1,0:T(8,128)(2,1)} %param.18) | copy-start | bytes 1769476
Sparse Core Ops, SparseCore 0:
  11.0 62.9 all-gather.6
  76.9 52.8 all-gather.8
  151.6 95.9 all-gather.12
  249.6 96.8 all-gather.10
  362.0 116.2 reduce-scatter.9
  481.7 117.2 reduce-scatter.7
  601.5 21.2 reduce-scatter.17
  625.3 22.0 reduce-scatter.15
  653.3 99.5 reduce-scatter.13
  759.0 118.5 reduce-scatter.11
where the time goes:
time: 894 us; the launch traced here: 885 us
  waiting for transfers between devices  541 us (61%)
  blocking collectives  149 us (17%)
  matrix products  112 us (13%)
  other arithmetic  32.3 us (4%)
  local copies, waits for them, and re-layouts  24.2 us (3%)
  between operations  15.5 us (2%)
  starting transfers between devices  10.9 us (1%)
    reduce_scatter x1, waiting for transfers between devices, shards(): lax.psum_scatter(grad_qkv_part, ('batch', 'wide'), scatter_dimension=0, t...  125 us
    reduce_scatter x1, waiting for transfers between devices, shards(): lax.psum_scatter(jnp.dot(piece, w_fc2, preferred_element_type=jnp.float32...  119 us
    all_gather x1, waiting for transfers between devices, shards(): lax.all_gather(normed_two[None], 'wide', axis=0, tiled=True)  93.8 us
    all_gather x1, waiting for transfers between devices, shards(): lax.all_gather(grad_out[None], 'wide', axis=0, tiled=True)  90.1 us
    unnamed x2, blocking collectives  82.8 us
    reduce_scatter x1, waiting for transfers between devices, shards(): lax.psum_scatter(contract_last(piece, w_in).astype(jnp.bfloat16), 'wide',...  79.5 us
    all_gather x1, blocking collectives, shards(): lax.all_gather(conv_taps, ('batch', 'wide'), axis=0, tiled=True)  66.4 us
    reduce_scatter x1, waiting for transfers between devices, shards(): lax.psum_scatter(grad_w_out_part, ('batch', 'wide'), scatter_dimension=0,...  32.6 us
  transfers between devices with their start and end apart: 10, of which 6 were waited for; matrix products, arithmetic and copies ran while one was open for 16% of the time, Pallas kernels for 0%

commit v1 on v0

--- a/solution.py
+++ b/solution.py
@@ -1,6 +1,9 @@
+import functools
 import jax
 import jax.numpy as jnp
 from jax import lax
+from jax.experimental import pallas as pl
+from jax.experimental.pallas import tpu as pltpu
 from jax.sharding import PartitionSpec as P
 
 HEADS = 12
@@ -199,32 +202,570 @@
     )
 
 
+BF = jnp.bfloat16
+F32 = jnp.float32
+AXES = ("batch", "wide")
+LANES = 256
+WIDE_PART = 256
+
+
+def fits(mesh, args):
+    inputs, w_qkv, w_in = args[0], args[3], args[8]
+    count = mesh.shape["batch"] * mesh.shape["wide"]
+    return (
+        mesh.shape["batch"] == 4
+        and mesh.shape["wide"] == 8
+        and inputs.shape[0] == count
+        and inputs.shape[1] % LANES == 0
+        and w_qkv.shape[0] % (count * 8) == 0
+        and w_qkv.shape[0] % LANES == 0
+        and w_qkv.shape[0] // HEADS == HD
+        and w_in.shape[1] == 8 * (WIDE_PART + WIDE_PART // 2)
+        and (w_in.shape[0] // 4) % 16 == 0
+    )
+
+
+def dot(left, right, left_dim, right_dim):
+    return lax.dot_general(
+        left, right, (((left_dim,), (right_dim,)), ((), ())), preferred_element_type=F32
+    )
+
+
+def flip_pairs(rule):
+    return [(i, i ^ rule(i)) for i in range(32)]
+
+
+def send(array, rule):
+    return lax.ppermute(array, AXES, flip_pairs(rule))
+
+
+def over_core(i):
+    return 8
+
+
+def over_first(i):
+    return 16 if i & 8 else 1
+
+
+def over_second(i):
+    return 1 if i & 8 else 16
+
+
+def over_z(step):
+    return lambda i: 2 * step
+
+
+def gather_blocks(block):
+    part = block[None]
+    part = jnp.concatenate([part] + [send(part, over_z(s)) for s in (1, 2, 3)])
+    part = jnp.concatenate([part, send(part, over_first)])
+    part = jnp.concatenate([part, send(part, over_second)])
+    return jnp.concatenate([part, send(part, over_core)])
+
+
+def scatter_core(keep, away):
+    return keep.astype(F32) + send(away, over_core).astype(F32)
+
+
+def scatter_rest(total, wire=BF):
+    for rule in (over_second, over_first):
+        half = total.shape[0] // 2
+        come = send(total[half:].astype(wire), rule)
+        total = total[:half] + come.astype(F32)
+    come = [send(total[s].astype(wire), over_z(s)) for s in (1, 2, 3)]
+    return total[0] + come[0].astype(F32) + come[1].astype(F32) + come[2].astype(F32)
+
+
+def place_of(me, other):
+    apart = me ^ other
+    x_bit, z_bits = apart & 1, (apart >> 1) & 3
+    core_bit, y_bit = (apart >> 3) & 1, (apart >> 4) & 1
+    on_first = ((other >> 3) & 1) == 0
+    high = jnp.where(on_first, y_bit, x_bit)
+    low = jnp.where(on_first, x_bit, y_bit)
+    return core_bit * 16 + high * 8 + low * 4 + z_bits
+
+
+def call(kernel, grid, in_specs, out_specs, out_shape, scratch=(), flops=0, nbytes=0, name=None, aliases=None):
+    return pl.pallas_call(
+        kernel,
+        grid_spec=pltpu.PrefetchScalarGridSpec(
+            num_scalar_prefetch=1,
+            grid=grid,
+            in_specs=in_specs,
+            out_specs=out_specs,
+            scratch_shapes=list(scratch),
+        ),
+        out_shape=out_shape,
+        compiler_params=pltpu.CompilerParams(
+            dimension_semantics=("arbitrary",) * len(grid), vmem_limit_bytes=60 * 1024 * 1024
+        ),
+        cost_estimate=pl.CostEstimate(flops=flops, bytes_accessed=nbytes, transcendentals=0),
+        name=name,
+        input_output_aliases=aliases or {},
+    )
+
+
+def whole(shape):
+    zeros = (0,) * len(shape)
+    return pl.BlockSpec(shape, lambda *_: zeros)
+
+
+def hat_of(values_in):
+    centered = values_in - jnp.mean(values_in, axis=-1, keepdims=True)
+    inv_std = lax.rsqrt(jnp.mean(centered * centered, axis=-1, keepdims=True) + epsilon)
+    return centered * inv_std, inv_std
+
+
+def turned(value):
+    return jnp.transpose(value.astype(F32)).astype(BF)
+
+
+def prepare_kernel(meta, cot_ref, go_ref, got_ref):
+    seq = cot_ref.shape[0]
+    quarter = got_ref.shape[1]
+    live = lax.broadcasted_iota(jnp.int32, (seq, 1), 0) < meta[33]
+    value = jnp.where(live, cot_ref[...].astype(F32), 0.0)
+    go_ref[...] = value.astype(BF)
+    flipped = jnp.transpose(value).astype(BF)
+    for b in range(4):
+        got_ref[b ^ meta[32]] = flipped[b * quarter : (b + 1) * quarter]
+
+
+def project_kernel(meta, x_ref, gain_ref, taps_ref, w_ref, proj_ref, mixed_ref, wn_ref, nt_ref, normed):
+    rows = w_ref.shape[1]
+
+    @pl.when(pl.program_id(0) == 0)
+    def _():
+        hat, _ = hat_of(x_ref[...].astype(F32))
+        low = (hat * gain_ref[...]).astype(BF)
+        normed[...] = low
+        flipped = turned(low)
+        for i in range(32):
+            nt_ref[meta[i]] = flipped[i * rows : (i + 1) * rows]
+
+    for i in range(32):
+        wn_ref[i * rows : (i + 1) * rows, :] = w_ref[meta[i]]
+    value = dot(normed[...], wn_ref[...], 1, 0)
+    at = lax.broadcasted_iota(jnp.int32, value.shape, 0)
+    one = jnp.where(at >= 1, pltpu.roll(value, 1, 0), 0.0)
+    two = jnp.where(at >= 2, pltpu.roll(value, 2, 0), 0.0)
+    mixed = value * taps_ref[0:1, :] + one * taps_ref[1:2, :] + two * taps_ref[2:3, :]
+    proj_ref[...] = value.astype(BF)
+    mixed_ref[...] = mixed.astype(BF)
+
+
+def head_row(head, scale=1.0):
+    lane = lax.broadcasted_iota(jnp.int32, (1, LANES), 1)
+    return jnp.where(lane // HD == head, scale, 0.0).astype(BF)
+
+
+def allowed_in(meta, keys, first_query, queries):
+    key = lax.broadcasted_iota(jnp.int32, (keys, queries), 0)
+    query = first_query + lax.broadcasted_iota(jnp.int32, (1, queries), 1)
+    return key < jnp.minimum(query + 1, meta[33])
+
+
+def attend_kernel(meta, q_ref, k_ref, v_ref, out_ref, lse_ref, flipped):
+    seq = q_ref.shape[0]
+    tile = LANES
+    values_t = turned(v_ref[...])
+    keys = k_ref[...]
+    for t in range(seq // tile):
+        upto = (t + 1) * tile
+        allowed = allowed_in(meta, upto, t * tile, tile)
+        query = q_ref[t * tile : upto, :]
+        for head in range(LANES // HD):
+            scores = dot(keys[:upto], query * head_row(head, 0.125), 1, 1)
+            scores = jnp.where(allowed, scores, -1e30)
+            top = jnp.max(scores, axis=0, keepdims=True)
+            terms = jnp.exp(scores - top)
+            total = jnp.sum(terms, axis=0, keepdims=True)
+            probs = (terms * (1.0 / total)).astype(BF)
+            flipped[head * HD : (head + 1) * HD, t * tile : upto] = dot(
+                values_t[head * HD : (head + 1) * HD, :upto], probs, 1, 0
+            )
+            lse_ref[0, head : head + 1, t * tile : upto] = top + jnp.log(total)
+    out_ref[...] = jnp.transpose(flipped[...]).astype(BF)
+
+
+def mend_kernel(meta, att_ref, blocks_ref, x_ref, gain_ref, res_ref, n2_ref, n2t_ref, at_ref, wn_ref, held, sem):
+    first = blocks_ref.shape[1] - held.shape[1]
+    copy = pltpu.make_async_copy(blocks_ref.at[:, pl.ds(first, held.shape[1]), :], held, sem)
+    copy.start()
+    flipped = turned(att_ref[...])
+    rows = at_ref.shape[1]
+    for i in range(32):
+        at_ref[meta[i]] = flipped[i * rows : (i + 1) * rows]
+    copy.wait()
+    lanes = held.shape[2]
+    for i in range(32):
+        for c in range(wn_ref.shape[1] // lanes):
+            wn_ref[i * rows : (i + 1) * rows, c * lanes : (c + 1) * lanes] = held[
+                meta[i], c * rows : (c + 1) * rows, :
+            ]
+    residual = x_ref[...].astype(F32) + dot(att_ref[...], wn_ref[...], 1, 0)
+    res_ref[...] = residual
+    hat, _ = hat_of(residual)
+    low = (hat * gain_ref[...]).astype(BF)
+    n2_ref[...] = low
+    flipped = turned(low)
+    quarter = n2t_ref.shape[1]
+    for b in range(4):
+        n2t_ref[b ^ meta[32]] = flipped[b * quarter : (b + 1) * quarter]
+
+
+def ffn_kernel(per_step, first, meta, n2_ref, go_ref, n2t_ref, got_ref, *refs):
+    tiles, refs = refs[: 4 * per_step], refs[4 * per_step :]
+    if not first:
+        branch_in, grad_in = refs[:2]
+        refs = refs[2:]
+    branch_ref, grad_ref, keep_ref, away_ref = refs
+    step = pl.program_id(0)
+
+    @pl.when(step == 0)
+    def _():
+        if first:
+            branch_ref[...] = jnp.zeros_like(branch_ref)
+            grad_ref[...] = jnp.zeros_like(grad_ref)
+        else:
+            branch_ref[...] = branch_in[...]
+            grad_ref[...] = grad_in[...]
+
+    quarter = tiles[0].shape[1] // 2
+    lanes = tiles[0].shape[2]
+
+    def joined(start):
+        columns = [
+            jnp.concatenate(
+                [tiles[4 * k + b][0, start : start + quarter, :] for b in range(4)], axis=0
+            )
+            for k in range(per_step)
+        ]
+        return columns[0] if per_step == 1 else jnp.concatenate(columns, axis=1)
+
+    w_up, w_down = joined(0), joined(quarter)
+    pre = jnp.maximum(dot(n2_ref[...], w_up, 1, 0), 0.0)
+    activ = (pre * pre).astype(BF)
+    grad_pre = (dot(go_ref[...], w_down, 1, 0) * 2.0 * pre).astype(BF)
+    branch_ref[...] += dot(activ, w_down, 1, 1)
+    grad_ref[...] += dot(grad_pre, w_up, 1, 1)
+    for start, result in (
+        (0, dot(n2t_ref[...], grad_pre, 1, 0)),
+        (quarter, dot(got_ref[...], activ, 1, 0)),
+    ):
+        for apart in range(4):
+            target = away_ref if apart & 1 else keep_ref
+            for k in range(per_step):
+                place = meta[(apart ^ meta[32]) * 8 + step * per_step + k] & 15
+                target[place, start : start + quarter, :] = result[
+                    apart * quarter : (apart + 1) * quarter, k * lanes : (k + 1) * lanes
+                ].astype(BF)
+
+
+def turn_kernel(meta, grad_ref, branch_ref, res_ref, gain_ref, go_ref, at_ref, wn_ref, out_ref, gres_ref, gatt_ref, ggain_ref, keep_ref, away_ref):
+    residual = res_ref[...]
+    seq = residual.shape[0]
+    live = lax.broadcasted_iota(jnp.int32, (seq, 1), 0) < meta[33]
+    out_ref[...] = jnp.where(live, residual + branch_ref[...], 0.0).astype(BF)
+    hat, inv_std = hat_of(residual)
+    grad = grad_ref[...]
+    ggain_ref[...] = jnp.sum(grad * hat, axis=0, keepdims=True)
+    scaled = grad * gain_ref[...]
+    mean_first = jnp.mean(scaled, axis=-1, keepdims=True)
+    mean_second = jnp.mean(scaled * hat, axis=-1, keepdims=True)
+    grad_res = go_ref[...].astype(F32) + inv_std * (scaled - mean_first - hat * mean_second)
+    gres_ref[...] = grad_res
+    low = grad_res.astype(BF)
+    gatt_ref[...] = dot(low, wn_ref[...], 1, 1).astype(BF)
+    result = dot(at_ref[...], low, 1, 0)
+    lanes = keep_ref.shape[2]
+    chunks = result.shape[1] // lanes
+    rows = keep_ref.shape[1] // chunks
+    for i in range(32):
+        target = away_ref if i >= 16 else keep_ref
+        for c in range(chunks):
+            target[i & 15, c * rows : (c + 1) * rows, :] = result[
+                i * rows : (i + 1) * rows, c * lanes : (c + 1) * lanes
+            ].astype(BF)
+
+
+def attend_back_kernel(
+    meta, q_ref, k_ref, v_ref, pq_ref, pk_ref, pv_ref, tq_ref, tk_ref, tv_ref, go_ref, out_ref, lse_ref,
+    gq_ref, gk_ref, gv_ref, dtq_ref, dtk_ref, dtv_ref, flipped,
+):
+    seq = q_ref.shape[0]
+    tile = LANES
+    keys, values = k_ref[...], v_ref[...]
+    keys_t = turned(keys)
+    delta_t = jnp.transpose(go_ref[...].astype(F32) * out_ref[...].astype(F32))
+    grad_keys = [jnp.zeros((tile, LANES), F32) for _ in range(seq // tile)]
+    grad_values = list(grad_keys)
+    for t in range(seq // tile):
+        upto = (t + 1) * tile
+        allowed = allowed_in(meta, upto, t * tile, tile)
+        query, grad = q_ref[t * tile : upto, :], go_ref[t * tile : upto, :]
+        for head in range(LANES // HD):
+            lanes = slice(head * HD, (head + 1) * HD)
+            query_h, grad_h = query * head_row(head, 0.125), grad * head_row(head)
+            delta = jnp.sum(delta_t[lanes, t * tile : upto], axis=0, keepdims=True)
+            scores = dot(keys[:upto], query_h, 1, 1)
+            lse = lse_ref[0, head : head + 1, t * tile : upto]
+            probs = jnp.where(allowed, jnp.exp(scores - lse), 0.0)
+            grad_scores = (probs * (dot(values[:upto], grad_h, 1, 1) - delta)).astype(BF)
+            flipped[lanes, t * tile : upto] = dot(keys_t[lanes, :upto], grad_scores, 1, 0) * 0.125
+            add_values = dot(probs.astype(BF), grad_h, 1, 0)
+            add_keys = dot(grad_scores, query_h, 1, 0)
+            for s in range(t + 1):
+                rows = slice(s * tile, (s + 1) * tile)
+                grad_values[s] += add_values[rows]
+                grad_keys[s] += add_keys[rows]
+    mixed = (
+        jnp.transpose(flipped[...]),
+        jnp.concatenate(grad_keys, axis=0),
+        jnp.concatenate(grad_values, axis=0),
+    )
+    at = lax.broadcasted_iota(jnp.int32, (seq, LANES), 0)
+    for grad, proj_ref, taps_ref, g_ref, dt_ref in zip(
+        mixed, (pq_ref, pk_ref, pv_ref), (tq_ref, tk_ref, tv_ref), (gq_ref, gk_ref, gv_ref), (dtq_ref, dtk_ref, dtv_ref)
+    ):
+        one = jnp.where(at < seq - 1, pltpu.roll(grad, seq - 1, 0), 0.0)
+        two = jnp.where(at < seq - 2, pltpu.roll(grad, seq - 2, 0), 0.0)
+        g_ref[...] = (grad * taps_ref[0:1, :] + one * taps_ref[1:2, :] + two * taps_ref[2:3, :]).astype(BF)
+        proj = proj_ref[...].astype(F32)
+        for tap, part in enumerate((grad, one, two)):
+            dt_ref[tap : tap + 1, :] = jnp.sum(part * proj, axis=0, keepdims=True)
+
+
+def weight_kernel(meta, nt_ref, gq_ref, gk_ref, gv_ref, keep_ref, away_ref):
+    start = pl.program_id(0) * LANES
+    width = keep_ref.shape[1] // 3
+    half = keep_ref.shape[0]
+    for part, g_ref in enumerate((gq_ref, gk_ref, gv_ref)):
+        result = dot(nt_ref[...], g_ref[...], 1, 0).astype(BF)
+        columns = pl.ds(pl.multiple_of(part * width + start, LANES), LANES)
+        keep_ref[:, columns] = result[:half]
+        away_ref[:, columns] = result[half:]
+
+
+def last_kernel(meta, gq_ref, gk_ref, gv_ref, wq_ref, wk_ref, wv_ref, x_ref, gain_ref, gres_ref, gin_ref, ggain_ref, total):
+    step = pl.program_id(0)
+    part = (
+        dot(gq_ref[...], wq_ref[...], 1, 1)
+        + dot(gk_ref[...], wk_ref[...], 1, 1)
+        + dot(gv_ref[...], wv_ref[...], 1, 1)
+    )
+
+    @pl.when(step == 0)
+    def _():
+        total[...] = part
+
+    @pl.when(step > 0)
+    def _():
+        total[...] += part
+
+    @pl.when(step == pl.num_programs(0) - 1)
+    def _():
+        hat, inv_std = hat_of(x_ref[...].astype(F32))
+        grad = total[...]
+        ggain_ref[...] = jnp.sum(grad * hat, axis=0, keepdims=True)
+        scaled = grad * gain_ref[...]
+        mean_first = jnp.mean(scaled, axis=-1, keepdims=True)
+        mean_second = jnp.mean(scaled * hat, axis=-1, keepdims=True)
+        back = inv_std * (scaled - mean_first - hat * mean_second)
+        gin_ref[...] = (gres_ref[...] + back).astype(BF)
+
+
+def own_sequence(inputs, lengths, cotangent, w_qkv, w_out, conv_taps, gain_one, gain_two, w_in, w_fc2):
+    seq, width = inputs.shape[1], inputs.shape[2]
+    rows = w_qkv.shape[0]
+    wide = w_qkv.shape[1]
+    quarter = width // 4
+    part_a, part_b = WIDE_PART, WIDE_PART // 2
+    batch = lax.axis_index("batch")
+    me = batch * 8 + lax.axis_index("wide")
+    number = jnp.arange(64, dtype=jnp.int32)
+    meta = jnp.where(number < 32, place_of(me, number & 31), jnp.where(number == 32, batch, lengths[0]))
+    natural = jax.nn.one_hot(meta[:32], 32, dtype=F32)
+    x, cot = inputs[0], cotangent[0]
+    shape = jax.ShapeDtypeStruct
+    row_spec = whole((1, width))
+
+    small = jnp.zeros((8, 128), BF)
+    small = small.at[:3, : conv_taps.shape[0]].set(conv_taps.T)
+    small = small.at[3, :rows].set(gain_one).at[4, :rows].set(gain_two)
+    small = gather_blocks(small)
+    small = jnp.einsum("dp,prl->drl", natural, small.astype(F32), precision="highest")
+    taps = jnp.transpose(small[:, :3, : conv_taps.shape[0]], (1, 0, 2)).reshape(3, wide)
+    taps = jnp.concatenate([taps, jnp.zeros((5, wide), F32)])
+    gain_first = small[:, 3, :rows].reshape(1, width)
+    gain_second = small[:, 4, :rows].reshape(1, width)
+    qkv_blocks = gather_blocks(w_qkv)
+    up = lax.dynamic_slice(w_in, (batch * quarter, 0), (quarter, part_a + part_b))
+    down = jnp.transpose(lax.dynamic_slice(w_fc2, (0, batch * quarter), (part_a + part_b, quarter)))
+    out_chunks = [w_out[:, c * part_a : (c + 1) * part_a] for c in range(width // part_a)]
+    blocks_a = gather_blocks(jnp.concatenate([up[:, :part_a], down[:, :part_a]] + out_chunks))
+    blocks_b = gather_blocks(jnp.concatenate([up[:, part_a:], down[:, part_a:]]))
+
+    grad_out, grad_out_t = call(
+        prepare_kernel, (1,), [whole((seq, width))], [whole((seq, width)), whole((4, quarter, seq))],
+        [shape((seq, width), BF), shape((4, quarter, seq), BF)], nbytes=3 * seq * width * 2, name="prepare",
+    )(meta, cot)
+    lane_block = pl.BlockSpec((seq, LANES), lambda j, m: (0, j))
+    projected, mixed, qkv_full, normed_t = call(
+        project_kernel, (wide // LANES,),
+        [whole((seq, width)), row_spec, pl.BlockSpec((8, LANES), lambda j, m: (0, j)),
+         pl.BlockSpec((32, rows, LANES), lambda j, m: (0, 0, j))],
+        [lane_block, lane_block, pl.BlockSpec((width, LANES), lambda j, m: (0, j)), whole((32, rows, seq))],
+        [shape((seq, wide), BF), shape((seq, wide), BF), shape((width, wide), BF), shape((32, rows, seq), BF)],
+        [pltpu.VMEM((seq, width), BF)], flops=2 * seq * width * wide, nbytes=12 * seq * width, name="project",
+    )(meta, x, gain_first, taps, qkv_blocks)
+    groups = width // LANES
+    part_specs = [pl.BlockSpec((seq, LANES), lambda j, m, p=p: (0, p * groups + j)) for p in range(3)]
+    lse_spec = pl.BlockSpec((1, 8, seq), lambda j, m: (j, 0, 0))
+    attended, lse = call(
+        attend_kernel, (groups,), part_specs, [lane_block, lse_spec],
+        [shape((seq, width), BF), shape((groups, 8, seq), F32)], [pltpu.VMEM((LANES, seq), F32)],
+        flops=4 * seq * seq * width, nbytes=8 * seq * width, name="attend",
+    )(meta, mixed, mixed, mixed)
+    out_rows = rows * (width // part_a)
+    residual, normed_two, normed_two_t, attended_t, out_full = call(
+        mend_kernel, (1,),
+        [whole((seq, width)), pl.BlockSpec(memory_space=pl.ANY), whole((seq, width)), row_spec],
+        [whole((seq, width)), whole((seq, width)), whole((4, quarter, seq)), whole((32, rows, seq)), whole((width, width))],
+        [shape((seq, width), F32), shape((seq, width), BF), shape((4, quarter, seq), BF), shape((32, rows, seq), BF),
+         shape((width, width), BF)],
+        [pltpu.VMEM((32, out_rows, part_a), BF), pltpu.SemaphoreType.DMA],
+        flops=2 * seq * width * width, nbytes=16 * seq * width, name="mend",
+    )(meta, attended, blocks_a, x, gain_second)
+
+    normed_two_t = normed_two_t.reshape(width, seq)
+    grad_out_t = grad_out_t.reshape(width, seq)
+    sums = ()
+    grads = []
+    for blocks, lanes in ((blocks_a, part_a), (blocks_b, part_b)):
+        per_step = LANES // lanes
+        first = not sums
+        tile_specs = [
+            pl.BlockSpec(
+                (1, 2 * quarter, lanes),
+                lambda s, m, b=b, k=k, n=per_step: (m[b * 8 + s * n + k], 0, 0),
+            )
+            for k in range(per_step)
+            for b in range(4)
+        ]
+        token = whole((seq, width))
+        grad_spec = whole((16, 2 * quarter, lanes))
+        *sums, keep, away = call(
+            functools.partial(ffn_kernel, per_step, first), (8 // per_step,),
+            [token, token, whole((width, seq)), whole((width, seq))] + tile_specs + [token] * len(sums),
+            [token, token, grad_spec, grad_spec],
+            [shape((seq, width), F32)] * 2 + [shape((16, 2 * quarter, lanes), BF)] * 2,
+            flops=12 * seq * width * lanes * 8, nbytes=8 * seq * width * 4, name="ffn",
+        )(meta, normed_two, grad_out, normed_two_t, grad_out_t, *[blocks] * (4 * per_step), *sums)
+        grads.append((keep, away))
+    branch, grad_normed_two = sums
+    grad_a = scatter_core(*grads[0])
+    chunk_rows = rows * (width // part_b)
+    output, grad_residual, grad_attended, grad_gain_second, keep_out, away_out = call(
+        turn_kernel, (1,),
+        [whole((seq, width))] * 3 + [row_spec, whole((seq, width)), whole((width, seq)), whole((width, width))],
+        [whole((seq, width))] * 3 + [row_spec, whole((16, chunk_rows, part_b)), whole((16, chunk_rows, part_b))],
+        [shape((seq, width), BF), shape((seq, width), F32), shape((seq, width), BF), shape((1, width), F32),
+         shape((16, chunk_rows, part_b), BF), shape((16, chunk_rows, part_b), BF)],
+        flops=4 * seq * width * width, nbytes=20 * seq * width, name="turn",
+    )(meta, grad_normed_two, branch, residual, gain_second, grad_out, attended_t.reshape(width, seq), out_full)
+    grad_a = scatter_rest(grad_a)
+    grad_b = jnp.concatenate([scatter_core(*grads[1]), scatter_core(keep_out, away_out)], axis=1)
+    grad_b = scatter_rest(grad_b)
+
+    tap_specs = [pl.BlockSpec((8, LANES), lambda j, m, p=p: (0, p * groups + j)) for p in range(3)]
+    tap_out = pl.BlockSpec((8, LANES), lambda j, m: (0, j))
+    *grad_projected, tap_q, tap_k, tap_v = call(
+        attend_back_kernel, (groups,),
+        part_specs * 2 + tap_specs + [lane_block, lane_block, lse_spec],
+        [lane_block] * 3 + [tap_out] * 3,
+        [shape((seq, width), BF)] * 3 + [shape((8, width), F32)] * 3,
+        [pltpu.VMEM((LANES, seq), F32)],
+        flops=10 * seq * seq * width, nbytes=24 * seq * width, name="attend_back",
+    )(meta, mixed, mixed, mixed, projected, projected, projected, taps, taps, taps, grad_attended, attended, lse)
+    half_spec = whole((width // 2, wide))
+    keep_qkv, away_qkv = call(
+        weight_kernel, (groups,), [whole((width, seq))] + [lane_block] * 3, [half_spec, half_spec],
+        [shape((width // 2, wide), BF)] * 2,
+        flops=2 * seq * width * wide, nbytes=8 * seq * width, name="weight",
+    )(meta, normed_t.reshape(width, seq), *grad_projected)
+    by_block = (16, rows, wide)
+    grad_qkv = scatter_rest(scatter_core(keep_qkv.reshape(by_block), away_qkv.reshape(by_block)))
+    weight_specs = [pl.BlockSpec((width, LANES), lambda j, m, p=p: (0, p * groups + j)) for p in range(3)]
+    grad_inputs, grad_gain_first = call(
+        last_kernel, (groups,),
+        [lane_block] * 3 + weight_specs + [whole((seq, width)), row_spec, whole((seq, width))],
+        [whole((seq, width)), row_spec], [shape((seq, width), BF), shape((1, width), F32)],
+        [pltpu.VMEM((seq, width), F32)],
+        flops=2 * seq * width * wide, nbytes=16 * seq * width, name="last",
+    )(meta, *grad_projected, qkv_full, qkv_full, qkv_full, x, gain_first, grad_residual)
+
+    tap_grads = jnp.concatenate([tap_q[:3], tap_k[:3], tap_v[:3]], axis=1)
+    tap_grads = jnp.transpose(tap_grads.reshape(3, 32, wide // 32), (1, 0, 2))
+    gain_grads = jnp.stack([grad_gain_first.reshape(32, rows), grad_gain_second.reshape(32, rows)], axis=1)
+    few = jnp.zeros((32, 8, 128), F32)
+    few = few.at[:, :3, : wide // 32].set(tap_grads).at[:, 3:5, :rows].set(gain_grads)
+    few = jnp.einsum("dp,drl->prl", natural, few, precision="highest")
+    few = scatter_rest(scatter_core(few[:16], few[16:]), F32)
+
+    ffn_a, ffn_b = grad_a, grad_b[: 2 * quarter]
+    grad_out_w = grad_b[2 * quarter :]
+    grad_out_w = jnp.concatenate(
+        [grad_out_w[c * rows : (c + 1) * rows] for c in range(width // part_b)], axis=1
+    )
+    grad_in_w = jnp.concatenate([ffn_a[:quarter], ffn_b[:quarter]], axis=1)
+    grad_fc2_w = jnp.transpose(jnp.concatenate([ffn_a[quarter:], ffn_b[quarter:]], axis=1))
+    return (
+        output[None],
+        grad_inputs[None],
+        grad_qkv,
+        grad_out_w,
+        few[:3, : wide // 32].T,
+        few[3, :rows],
+        few[4, :rows],
+        grad_in_w,
+        grad_fc2_w,
+    )
+
+
 def solution(mesh):
-    return jax.shard_map(
-        shards,
-        mesh=mesh,
-        in_specs=(
-            P(("batch", "wide"), None, None),
-            P(("batch", "wide")),
-            P(("batch", "wide"), None, None),
-            P(("batch", "wide"), None),
-            P(("batch", "wide"), None),
-            P(("batch", "wide"), None),
-            P(("batch", "wide")),
-            P(("batch", "wide")),
-            P(None, "wide"),
-            P("wide", None),
-        ),
-        out_specs=(
-            P(("batch", "wide"), None, None),
-            P(("batch", "wide"), None, None),
-            P(("batch", "wide"), None),
-            P(("batch", "wide"), None),
-            P(("batch", "wide"), None),
-            P(("batch", "wide")),
-            P(("batch", "wide")),
-            P("batch", "wide"),
-            P("wide", "batch"),
-        ),
-        check_vma=False,
-    )
+    fast = functools.partial(own_sequence)
+
+    def program(*args):
+        body = fast if fits(mesh, args) else shards
+        return jax.shard_map(
+            body,
+            mesh=mesh,
+            in_specs=(
+                P(("batch", "wide"), None, None),
+                P(("batch", "wide")),
+                P(("batch", "wide"), None, None),
+                P(("batch", "wide"), None),
+                P(("batch", "wide"), None),
+                P(("batch", "wide"), None),
+                P(("batch", "wide")),
+                P(("batch", "wide")),
+                P(None, "wide"),
+                P("wide", None),
+            ),
+            out_specs=(
+                P(("batch", "wide"), None, None),
+                P(("batch", "wide"), None, None),
+                P(("batch", "wide"), None),
+                P(("batch", "wide"), None),
+                P(("batch", "wide"), None),
+                P(("batch", "wide")),
+                P(("batch", "wide")),
+                P("batch", "wide"),
+                P("wide", "batch"),
+            ),
+            check_vma=False,
+        )(*args)
+
+    return program

time: 894 us -> 348 us (0.39)
  waiting for transfers between devices: 541 us -> 124 us
  blocking collectives: 149 us -> 0 us
  matrix products: 112 us -> 1.06 us
  Pallas kernels: 0 us -> 100 us
  starting transfers between devices: 10.9 us -> 67.5 us
  other arithmetic: 32.3 us -> 10.7 us
  local copies, waits for them, and re-layouts: 24.2 us -> 41.2 us
  between operations: 15.5 us -> 2 us
    reduce_scatter x6 -> x0, waiting for transfers between devices: 356 us -> none  [the longest x1 125 us: shards(): lax.psum_scatter(grad_qkv_part, ('batch', 'wide'), scatter_dimension=0, t...]
    all_gather x4 -> x0, waiting for transfers between devices: 184 us -> none  [the longest x1 93.8 us: shards(): lax.all_gather(normed_two[None], 'wide', axis=0, tiled=True)]
    ppermute x0 -> x49, waiting for transfers between devices: none -> 124 us  [send(): return lax.ppermute(array, AXES, flip_pairs(rule))]
    dot_general x18 -> x2, matrix products: 112 us -> 1.06 us  [the longest x1 0.86 us: own_sequence(): jnp.einsum('dp,prl->drl', natural, small.astype(F32), precision='highest')]
    pallas_call x0 -> x10, Pallas kernels: none -> 100 us  [the longest x2 31.3 us: own_sequence(): call(functools.partial(ffn_kernel, per_step, first), (8 // per_step,), [t...]
    unnamed x2 -> x0, blocking collectives: 82.8 us -> none
    ppermute x0 -> x49, starting transfers between devices: none -> 67.5 us  [send(): return lax.ppermute(array, AXES, flip_pairs(rule))]
    all_gather x1 -> x0, blocking collectives: 66.4 us -> none  [shards(): lax.all_gather(conv_taps, ('batch', 'wide'), axis=0, tiled=True)]
  transfers between devices with their start and end apart: 10 -> 49, of which waited for: 6 -> 25; matrix products, arithmetic and copies ran while one was open for 16% -> 12% of each run, Pallas kernels for 0% -> 7%
where the time goes in v1:
time: 348 us; the launch traced here: 347 us
  waiting for transfers between devices  124 us (36%)
  Pallas kernels  100 us (29%)
  starting transfers between devices  67.5 us (19%)
  local copies, waits for them, and re-layouts  41.2 us (12%)
  other arithmetic  10.7 us (3%)
    ppermute x49, waiting for transfers between devices, send(): return lax.ppermute(array, AXES, flip_pairs(rule))  124 us
    ppermute x49, starting transfers between devices, send(): return lax.ppermute(array, AXES, flip_pairs(rule))  67.5 us
    pallas_call x2, Pallas kernels, own_sequence(): call(functools.partial(ffn_kernel, per_step, first), (8 // per_step,), [t...  31.3 us
    unnamed x59, local copies, waits for them, and re-layouts  19.9 us
    pallas_call x1, Pallas kernels, own_sequence(): call(attend_back_kernel, (groups,), part_specs * 2 + tap_specs + [lane_bl...  15 us
    pallas_call x1, Pallas kernels, own_sequence(): call(project_kernel, (wide // LANES,), [whole((seq, width)), row_spec, pl...  11.3 us
    pallas_call x1, Pallas kernels, own_sequence(): call(attend_kernel, (groups,), part_specs, [lane_block, lse_spec], [shape...  10.9 us
    concatenate x4, local copies, waits for them, and re-layouts, gather_blocks(): return jnp.concatenate([part, send(part, over_core)])  9.87 us
  transfers between devices with their start and end apart: 49, of which 25 were waited for; matrix products, arithmetic and copies ran while one was open for 12% of the time, Pallas kernels for 7%

profile of v1, /device:TPU:0, one launch (start us, length us, event | category | flops | bytes accessed | tf_op | source)
XLA Modules:
  0.0 346.7 jit_solution(15465743497394848449)
XLA Ops:
  5.0 3.1 collective-permute-start.12
  8.1 2.6 collective-permute-start.13
  11.6 3.5 %collective-permute-start.7 = (bf16[1,24,2304]{2,1,0:T(8,128)(2,1)}, bf16[1,24,2304]{2,1,0:T(8,128)(2,1)}, u32[]{:S(2)}, u32[]{:S(2)}) collective-permute-start(bf16[1,24,2304]{2,1,0:T(8,128)(2,1)} %bitcast.135), channel_id=1, source_target_pairs={{0,4},{1,5},{2,6},{3,7},{4,0},{5,1},{6,2},{7,3},{8,12},{9,13},{10,... | collective-permute-start | bytes 331784 | tf_op jit(solution)/shard_map/ppermute | solution.py:239
  17.4 1.6 collective-permute-done.12
  19.0 9.0 %collective-permute-done.13 = bf16[1,456,256]{2,1,0:T(8,128)(2,1)} collective-permute-done((bf16[1,456,256]{2,1,0:T(8,128)(2,1)S(1)}, bf16[1,456,256]{2,1,0:T(8,128)(2,1)}, u32[]{:S(2)}, u32[]{:S(2)}) %collective-permute-start.13) | collective-permute-done | bytes 233504 | tf_op jit(solution)/shard_map/ppermute | solution.py:239
  29.3 1.6 collective-permute-start.15
  31.6 1.8 constant_dynamic-update-slice_fusion.32
  33.3 1.8 constant_dynamic-update-slice_fusion.31
  35.1 1.8 constant_dynamic-update-slice_fusion.30
  36.9 6.0 %collective-permute-done.15 = bf16[4,456,256]{2,1,0:T(8,128)(2,1)S(1)} collective-permute-done((bf16[4,456,256]{2,1,0:T(8,128)(2,1)S(1)}, bf16[4,456,256]{2,1,0:T(8,128)(2,1)S(1)}, u32[]{:S(2)}, u32[]{:S(2)}) %collective-permute-start.15) | collective-permute-done | bytes 933920 | tf_op jit(solution)/shard_map/ppermute | solution.py:239
  42.9 3.7 %collective-permute-start.20 = (bf16[1,384,128]{2,1,0:T(8,128)(2,1)S(1)}, bf16[1,384,128]{2,1,0:T(8,128)(2,1)S(1)}, u32[]{:S(2)}, u32[]{:S(2)}) collective-permute-start(bf16[1,384,128]{2,1,0:T(8,128)(2,1)S(1)} %maximum_bitcast_fusion.1), channel_id=1, source_target_pairs={{0,6},{1,7},{2,4},{3,5},{4,2},{5,3},{6,0},{7,1},{8,14},{9,15},{10,... | collective-permute-start | bytes 294920 | tf_op jit(solution)/shard_map/ppermute | solution.py:239
  49.8 1.6 collective-permute-start.21
  51.3 3.4 collective-permute-done.8
  55.7 1.6 collective-permute-start.9
  57.3 1.6 constant_dynamic-update-slice_fusion.9
  58.9 1.6 constant_dynamic-update-slice_fusion.8
  61.2 10.1 %collective-permute-done.9 = bf16[4,24,2304]{2,1,0:T(8,128)(2,1)S(1)} collective-permute-done((bf16[4,24,2304]{2,1,0:T(8,128)(2,1)S(1)}, bf16[4,24,2304]{2,1,0:T(8,128)(2,1)S(1)}, u32[]{:S(2)}, u32[]{:S(2)}) %collective-permute-start.9) | collective-permute-done | bytes 442400 | tf_op jit(solution)/shard_map/ppermute | solution.py:239
  73.5 3.4 collective-permute-done.16
  76.9 2.1 constant_dynamic-update-slice_fusion.28
  83.5 3.0 collective-permute-done.10
  87.8 7.1 %collective-permute-done.22 = bf16[8,384,128]{2,1,0:T(8,128)(2,1)S(1)} collective-permute-done((bf16[8,384,128]{2,1,0:T(8,128)(2,1)S(1)}, bf16[8,384,128]{2,1,0:T(8,128)(2,1)S(1)}, u32[]{:S(2)}, u32[]{:S(2)}) %collective-permute-start.22) | collective-permute-done | bytes 786464 | tf_op jit(solution)/shard_map/ppermute | solution.py:239
  96.6 8.0 %collective-permute-start = (bf16[1,8,128]{2,0,1:T(2,128)(2,1)S(1)}, bf16[1,8,128]{2,0,1:T(2,128)(2,1)S(1)}, u32[]{:S(2)}, u32[]{:S(2)}) collective-permute-start(bf16[1,8,128]{2,0,1:T(2,128)(2,1)S(1)} %scatter.20), channel_id=1, source_target_pairs={{0,2},{1,3},{2,0},{3,1},{4,6},{5,7},{6,4},{7,5},{8,10},{9,11},{10,... | collective-permute-start | bytes 6152 | tf_op jit(solution)/shard_map/ppermute | solution.py:239
  104.6 1.6 collective-permute-start.1
  106.2 3.0 collective-permute-start.2
  109.2 2.5 collective-permute-done.2
  113.2 2.2 collective-permute-done.3
  115.4 1.6 collective-permute-start.4
  117.6 1.6 collective-permute-done.4
  119.9 3.2 prepare.1
  126.1 1.7 constant_dynamic-update-slice_fusion.52.refs_0_.refs_1_.refs_2_.refs_3_.refs_4_.refs_5_.refs_6_.refs_7_
  127.8 4.0 %constant_dynamic-update-slice_fusion.11.w_ref = bf16[32,24,2304]{2,1,0:T(8,128)(2,1)} fusion(bf16[32,24,2304]{2,1,0:T(8,128)(2,1)} %get-tuple-element.155, bf16[16,24,2304]{2,1,0:T(8,128)(2,1)} %collective-permute-done.11), kind=kLoop, calls=%fused_computation.54 | loop fusion | bytes 3538944 | tf_op jit(solution)/shard_map/concatenate | solution.py:263
  131.7 11.3 %project.1 = (bf16[512,2304]{1,0:T(8,128)(2,1)}, bf16[512,2304]{1,0:T(8,128)(2,1)}, bf16[768,2304]{1,0:T(8,128)(2,1)}, bf16[32,24,512]{2,1,0:T(8,128)(2,1)}) custom-call(s32[64]{0:T(128)} %compare_select_fusion.1.meta, bf16[512,768]{1,0:T(8,128)(2,1)} %bitcast.118, f32[1,768]{1,0:T(1,128)} %reshape_squeeze.6.gain_ref, ...), custom_call_target="tpu_custom_call" | custom-call | flops 1811939328 | bytes 4718592 | tf_op jit(solution)/shard_map/project/pallas_call | solution.py:615
  143.1 10.9 %attend.1 = (bf16[512,768]{1,0:T(8,128)(2,1)}, f32[3,8,512]{2,1,0:T(8,128)}) custom-call(s32[64]{0:T(128)} %compare_select_fusion.1.meta, bf16[512,2304]{1,0:T(8,128)(2,1)} %get-tuple-element.106.q_ref.k_ref.v_ref, bf16[512,2304]{1,0:T(8,128)(2,1)} %get-tuple-element.106.q_ref.k_ref.v_ref, bf16[512,2304]{1,0:T(8,128)(2,1)} %get-tuple-element.106.q_ref.k_ref.v_ref), custom_call_target="tpu_custom_call" | custom-call | flops 805306368 | bytes 3145728 | tf_op jit(solution)/shard_map/attend/pallas_call | solution.py:626
  154.0 4.2 %constant_dynamic-update-slice_fusion.34.blocks_ref.refs_0_.refs_1_.refs_2_.refs_3_ = bf16[32,456,256]{2,1,0:T(8,128)(2,1)} fusion(bf16[32,456,256]{2,1,0:T(8,128)(2,1)} %get-tuple-element.150, bf16[16,456,256]{2,1,0:T(8,128)(2,1)} %collective-permute-done.17), kind=kLoop, calls=%fused_computation.77 | loop fusion | bytes 7471104 | tf_op jit(solution)/shard_map/concatenate | solution.py:263
  158.2 6.3 %mend.1 = (f32[512,768]{1,0:T(8,128)}, bf16[512,768]{1,0:T(8,128)(2,1)}, bf16[4,192,512]{2,1,0:T(8,128)(2,1)}, bf16[32,24,512]{2,1,0:T(8,128)(2,1)}, bf16[768,768]{1,0:T(8,128)(2,1)}) custom-call(s32[64]{0:T(128)} %compare_select_fusion.1.meta, bf16[512,768]{1,0:T(8,128)(2,1)} %get-tuple-element.107.att_ref.out_ref, ...), custom_call_target="tpu_custom_call" | custom-call | flops 603979776 | bytes 6291456 | tf_op jit(solution)/shard_map/mend/pallas_call | solution.py:632
  164.5 18.4 %ffn.2 = (f32[512,768]{1,0:T(8,128)}, f32[512,768]{1,0:T(8,128)}, bf16[16,384,256]{2,1,0:T(8,128)(2,1)}, bf16[16,384,256]{2,1,0:T(8,128)(2,1)}) custom-call(s32[64]{0:T(128)} %compare_select_fusion.1.meta, bf16[512,768]{1,0:T(8,128)(2,1)} %get-tuple-element.108.n2_ref, bf16[512,768]{1,0:T(8,128)(2,1)} %get-tuple-element.109.go_ref, ...), custom_call_target="tpu_custom_call" | custom-call | flops 9663676416 | bytes 12582912 | tf_op jit(solution)/shard_map/ffn/pallas_call | solution.py:659
  182.9 12.8 %ffn.3 = (f32[512,768]{1,0:T(8,128)}, f32[512,768]{1,0:T(8,128)}, bf16[16,384,128]{2,1,0:T(8,128)(2,1)}, bf16[16,384,128]{2,1,0:T(8,128)(2,1)}) custom-call(s32[64]{0:T(128)} %compare_select_fusion.1.meta, bf16[512,768]{1,0:T(8,128)(2,1)} %get-tuple-element.108.n2_ref, bf16[512,768]{1,0:T(8,128)(2,1)} %get-tuple-element.109.go_ref, ...), custom_call_target="tpu_custom_call" | custom-call | flops 4831838208 | bytes 12582912 | tf_op jit(solution)/shard_map/ffn/pallas_call | solution.py:659
  195.7 7.1 %turn.1 = (bf16[512,768]{1,0:T(8,128)(2,1)}, f32[512,768]{1,0:T(8,128)}, bf16[512,768]{1,0:T(8,128)(2,1)}, f32[1,768]{1,0:T(1,128)}, bf16[16,144,128]{2,1,0:T(8,128)(2,1)}, /*index=5*/bf16[16,144,128]{2,1,0:T(8,128)(2,1)}) custom-call(s32[64]{0:T(128)} %compare_select_fusion.1.meta, f32[512,768]{1,0:T(8,128)} %get-tuple-element.114.grad_ref, ...), custom_call_target="tpu_custom_call" | custom-call | flops 1207959552 | bytes 7864320 | tf_op jit(solution)/shard_map/turn/pallas_call | solution.py:670
  202.8 15.0 %attend_back.1 = (bf16[512,768]{1,0:T(8,128)(2,1)}, bf16[512,768]{1,0:T(8,128)(2,1)}, bf16[512,768]{1,0:T(8,128)(2,1)}, f32[8,768]{1,0:T(8,128)}, f32[8,768]{1,0:T(8,128)}, /*index=5*/f32[8,768]{1,0:T(8,128)}) custom-call(s32[64]{0:T(128)} %compare_select_fusion.1.meta, bf16[512,2304]{1,0:T(8,128)(2,1)} %get-tuple-element.106.q_ref.k_ref.v_ref, ...), custom_call_target="tpu_custom_call" | custom-call | flops 2013265920 | bytes 9437184 | tf_op jit(solution)/shard_map/attend_back/pallas_call | solution.py:684
  217.9 8.7 %last.1 = (bf16[512,768]{1,0:T(8,128)(2,1)}, f32[1,768]{1,0:T(1,128)}) custom-call(s32[64]{0:T(128)} %compare_select_fusion.1.meta, bf16[512,768]{1,0:T(8,128)(2,1)} %get-tuple-element.123.gq_ref, bf16[512,768]{1,0:T(8,128)(2,1)} %get-tuple-element.124.gk_ref, bf16[512,768]{1,0:T(8,128)(2,1)} %get-tuple-element.125.gv_ref, ...), custom_call_target="tpu_custom_call" | custom-call | flops 1811939328 | bytes 6291456 | tf_op jit(solution)/shard_map/last/pallas_call | solution.py:701
  227.7 6.7 %weight.1 = (bf16[384,2304]{1,0:T(8,128)(2,1)}, bf16[384,2304]{1,0:T(8,128)(2,1)}) custom-call(s32[64]{0:T(128)} %compare_select_fusion.1.meta, bf16[768,512]{1,0:T(8,128)(2,1)} %bitcast.147, bf16[512,768]{1,0:T(8,128)(2,1)} %get-tuple-element.123.gq_ref, bf16[512,768]{1,0:T(8,128)(2,1)} %get-tuple-element.124.gk_ref, bf16[512,768]{1,0:T(8,128)(2,1)} %get-tuple-element.125.gv_ref), custom_call_target="tpu_custom_call" | custom-call | flops 1811939328 | bytes 3145728 | tf_op jit(solution)/shard_map/weight/pallas_call | solution.py:693
  235.7 2.7 collective-permute-done.37
  238.5 1.6 collective-permute-start.38
  240.1 2.4 collective-permute-done.38
  242.5 1.5 collective-permute-start.39
  244.1 2.3 collective-permute-done.39
  246.6 3.2 collective-permute-start.41
  251.5 3.8 %collective-permute-done.42 = f32[8,128]{1,0:T(8,128)S(1)} collective-permute-done((f32[8,128]{1,0:T(8,128)S(1)}, f32[8,128]{1,0:T(8,128)S(1)}, u32[]{:S(2)}, u32[]{:S(2)}) %collective-permute-start.42) | collective-permute-done | bytes 4128 | tf_op jit(solution)/shard_map/ppermute | solution.py:239
  255.3 1.9 convert_add_fusion.1
  257.3 1.6 collective-permute-start.25
  261.3 10.4 %collective-permute-done.25 = bf16[8,24,2304]{2,1,0:T(8,128)(2,1)S(1)} collective-permute-done((bf16[8,24,2304]{2,1,0:T(8,128)(2,1)S(1)}, bf16[8,24,2304]{2,1,0:T(8,128)(2,1)S(1)}, u32[]{:S(2)}, u32[]{:S(2)}) %collective-permute-start.25) | collective-permute-done | bytes 884768 | tf_op jit(solution)/shard_map/ppermute | solution.py:239
  271.9 1.6 collective-permute-start.26
  274.0 16.5 %collective-permute-done.32 = bf16[8,528,128]{2,1,0:T(8,128)(2,1)S(1)} collective-permute-done((bf16[8,528,128]{2,1,0:T(8,128)(2,1)S(1)}, bf16[8,528,128]{2,1,0:T(8,128)(2,1)S(1)}, u32[]{:S(2)}, u32[]{:S(2)}) %collective-permute-start.32) | collective-permute-done | bytes 1081376 | tf_op jit(solution)/shard_map/ppermute | solution.py:239
  290.8 1.6 collective-permute-start.33
  292.6 4.3 %collective-permute-start.29 = (bf16[24,2304]{1,0:T(8,128)(2,1)S(1)}, bf16[24,2304]{1,0:T(8,128)(2,1)S(1)}, u32[]{:S(2)}, u32[]{:S(2)}) collective-permute-start(bf16[24,2304]{1,0:T(8,128)(2,1)S(1)} %get-tuple-element.165), channel_id=1, source_target_pairs={{0,6},{1,7},{2,4},{3,5},{4,2},{5,3},{6,0},{7,1},{8,14},{9,15},{10,... | collective-permute-start | bytes 331784 | tf_op jit(solution)/shard_map/ppermute | solution.py:239
  298.0 1.6 collective-permute-start.44
  299.6 6.4 %collective-permute-done.33 = bf16[4,528,128]{2,1,0:T(8,128)(2,1)S(1)} collective-permute-done((bf16[4,528,128]{2,1,0:T(8,128)(2,1)S(1)}, bf16[4,528,128]{2,1,0:T(8,128)(2,1)S(1)}, u32[]{:S(2)}, u32[]{:S(2)}) %collective-permute-start.33) | collective-permute-done | bytes 540704 | tf_op jit(solution)/shard_map/ppermute | solution.py:239
  306.4 4.3 %collective-permute-start.36 = (bf16[528,128]{1,0:T(8,128)(2,1)S(1)}, bf16[528,128]{1,0:T(8,128)(2,1)S(1)}, u32[]{:S(2)}, u32[]{:S(2)}) collective-permute-start(bf16[528,128]{1,0:T(8,128)(2,1)S(1)} %get-tuple-element.162), channel_id=1, source_target_pairs={{0,6},{1,7},{2,4},{3,5},{4,2},{5,3},{6,0},{7,1},{8,14},{9,15},{10,... | collective-permute-start | bytes 405512 | tf_op jit(solution)/shard_map/ppermute | solution.py:239
  312.7 2.5 collective-permute-done.35
  315.3 3.9 %collective-permute-done.44 = bf16[8,384,256]{2,1,0:T(8,128)(2,1)S(1)} collective-permute-done((bf16[8,384,256]{2,1,0:T(8,128)(2,1)S(1)}, bf16[8,384,256]{2,1,0:T(8,128)(2,1)S(1)}, u32[]{:S(2)}, u32[]{:S(2)}) %collective-permute-start.44) | collective-permute-done | bytes 1572896 | tf_op jit(solution)/shard_map/ppermute | solution.py:239
  319.8 11.9 %collective-permute-done.45 = bf16[4,384,256]{2,1,0:T(8,128)(2,1)S(1)} collective-permute-done((bf16[4,384,256]{2,1,0:T(8,128)(2,1)S(1)}, bf16[4,384,256]{2,1,0:T(8,128)(2,1)S(1)}, u32[]{:S(2)}, u32[]{:S(2)}) %collective-permute-start.45) | collective-permute-done | bytes 786464 | tf_op jit(solution)/shard_map/ppermute | solution.py:239
  333.1 3.4 collective-permute-start.48
  336.5 3.4 collective-permute-done.46
  339.9 5.9 %collective-permute-done.47 = bf16[384,256]{1,0:T(8,128)(2,1)S(1)} collective-permute-done((bf16[384,256]{1,0:T(8,128)(2,1)S(1)}, bf16[384,256]{1,0:T(8,128)(2,1)S(1)}, u32[]{:S(2)}, u32[]{:S(2)}) %collective-permute-start.47) | collective-permute-done | bytes 196640 | tf_op jit(solution)/shard_map/ppermute | solution.py:239
  (183 shorter events, 43.9 us)
Async XLA Ops:
  1.7 29.1 %copy-start.6 = (bf16[24,2304]{1,0:T(8,128)(2,1)S(1)}, bf16[24,2304]{1,0:T(8,128)(2,1)}, u32[]{:S(2)}) copy-start(bf16[24,2304]{1,0:T(8,128)(2,1)} %param.23) | copy-start | bytes 331780
  5.0 14.0 %collective-permute-start.12 = (bf16[1,456,256]{2,1,0:T(8,128)(2,1)S(1)}, bf16[1,456,256]{2,1,0:T(8,128)(2,1)}, u32[]{:S(2)}, u32[]{:S(2)}) collective-permute-start(bf16[1,456,256]{2,1,0:T(8,128)(2,1)S(1)} %bitcast.122), channel_id=1, source_target_pairs={{0,2},{1,3},{2,0},{3,1},{4,6},{5,7},{6,4},{7,5},{8,10},{9,11},{10,... | collective-permute-start | bytes 700424 | tf_op jit(solution)/shard_map/ppermute | solution.py:239
  8.1 19.9 %collective-permute-start.13 = (bf16[1,456,256]{2,1,0:T(8,128)(2,1)S(1)}, bf16[1,456,256]{2,1,0:T(8,128)(2,1)}, u32[]{:S(2)}, u32[]{:S(2)}) collective-permute-start(bf16[1,456,256]{2,1,0:T(8,128)(2,1)S(1)} %bitcast.123), channel_id=1, source_target_pairs={{0,4},{1,5},{2,6},{3,7},{4,0},{5,1},{6,2},{7,3},{8,12},{9,13},{10,... | collective-permute-start | bytes 700424 | tf_op jit(solution)/shard_map/ppermute | solution.py:239
  10.7 17.3 %collective-permute-start.14 = (bf16[1,456,256]{2,1,0:T(8,128)(2,1)S(1)}, bf16[1,456,256]{2,1,0:T(8,128)(2,1)}, u32[]{:S(2)}, u32[]{:S(2)}) collective-permute-start(bf16[1,456,256]{2,1,0:T(8,128)(2,1)S(1)} %bitcast.124), channel_id=1, source_target_pairs={{0,6},{1,7},{2,4},{3,5},{4,2},{5,3},{6,0},{7,1},{8,14},{9,15},{10,... | collective-permute-start | bytes 700424 | tf_op jit(solution)/shard_map/ppermute | solution.py:239
  10.7 40.7 %collective-permute-start.6 = (bf16[1,24,2304]{2,1,0:T(8,128)(2,1)}, bf16[1,24,2304]{2,1,0:T(8,128)(2,1)}, u32[]{:S(2)}, u32[]{:S(2)}) collective-permute-start(bf16[1,24,2304]{2,1,0:T(8,128)(2,1)} %bitcast.134), channel_id=1, source_target_pairs={{0,2},{1,3},{2,0},{3,1},{4,6},{5,7},{6,4},{7,5},{8,10},{9,11},{10,... | collective-permute-start | bytes 331784 | tf_op jit(solution)/shard_map/ppermute | solution.py:239
  11.6 39.8 %collective-permute-start.7 = (bf16[1,24,2304]{2,1,0:T(8,128)(2,1)}, bf16[1,24,2304]{2,1,0:T(8,128)(2,1)}, u32[]{:S(2)}, u32[]{:S(2)}) collective-permute-start(bf16[1,24,2304]{2,1,0:T(8,128)(2,1)} %bitcast.135), channel_id=1, source_target_pairs={{0,4},{1,5},{2,6},{3,7},{4,0},{5,1},{6,2},{7,3},{8,12},{9,13},{10,... | collective-permute-start | bytes 331784 | tf_op jit(solution)/shard_map/ppermute | solution.py:239
  19.0 29.1 %collective-permute-start.18 = (bf16[1,384,128]{2,1,0:T(8,128)(2,1)S(1)}, bf16[1,384,128]{2,1,0:T(8,128)(2,1)S(1)}, u32[]{:S(2)}, u32[]{:S(2)}) collective-permute-start(bf16[1,384,128]{2,1,0:T(8,128)(2,1)S(1)} %maximum_bitcast_fusion.1), channel_id=1, source_target_pairs={{0,2},{1,3},{2,0},{3,1},{4,6},{5,7},{6,4},{7,5},{8,10},{9,11},{10,... | collective-permute-start | bytes 294920 | tf_op jit(solution)/shard_map/ppermute | solution.py:239
  28.0 20.2 %collective-permute-start.19 = (bf16[1,384,128]{2,1,0:T(8,128)(2,1)S(1)}, bf16[1,384,128]{2,1,0:T(8,128)(2,1)S(1)}, u32[]{:S(2)}, u32[]{:S(2)}) collective-permute-start(bf16[1,384,128]{2,1,0:T(8,128)(2,1)S(1)} %maximum_bitcast_fusion.1), channel_id=1, source_target_pairs={{0,4},{1,5},{2,6},{3,7},{4,0},{5,1},{6,2},{7,3},{8,12},{9,13},{10,... | collective-permute-start | bytes 294920 | tf_op jit(solution)/shard_map/ppermute | solution.py:239
  29.3 13.6 %collective-permute-start.15 = (bf16[4,456,256]{2,1,0:T(8,128)(2,1)S(1)}, bf16[4,456,256]{2,1,0:T(8,128)(2,1)S(1)}, u32[]{:S(2)}, u32[]{:S(2)}) collective-permute-start(bf16[4,456,256]{2,1,0:T(8,128)(2,1)S(1)} %pad_maximum_fusion.1), channel_id=1, source_target_pairs={{0,1},{1,0},{2,3},{3,2},{4,5},{5,4},{6,7},{7,6},{8,24},{9,25},{10,... | collective-permute-start | bytes 2801672 | tf_op jit(solution)/shard_map/ppermute | solution.py:239
  42.9 6.8 %collective-permute-start.20 = (bf16[1,384,128]{2,1,0:T(8,128)(2,1)S(1)}, bf16[1,384,128]{2,1,0:T(8,128)(2,1)S(1)}, u32[]{:S(2)}, u32[]{:S(2)}) collective-permute-start(bf16[1,384,128]{2,1,0:T(8,128)(2,1)S(1)} %maximum_bitcast_fusion.1), channel_id=1, source_target_pairs={{0,6},{1,7},{2,4},{3,5},{4,2},{5,3},{6,0},{7,1},{8,14},{9,15},{10,... | collective-permute-start | bytes 294920 | tf_op jit(solution)/shard_map/ppermute | solution.py:239
  48.1 6.6 %collective-permute-start.8 = (bf16[1,24,2304]{2,1,0:T(8,128)(2,1)S(1)}, bf16[1,24,2304]{2,1,0:T(8,128)(2,1)S(1)}, u32[]{:S(2)}, u32[]{:S(2)}) collective-permute-start(bf16[1,24,2304]{2,1,0:T(8,128)(2,1)S(1)} %bitcast.136), channel_id=1, source_target_pairs={{0,6},{1,7},{2,4},{3,5},{4,2},{5,3},{6,0},{7,1},{8,14},{9,15},{10,... | collective-permute-start | bytes 331784 | tf_op jit(solution)/shard_map/ppermute | solution.py:239
  48.2 28.7 %collective-permute-start.16 = (bf16[8,456,256]{2,1,0:T(8,128)(2,1)S(1)}, bf16[8,456,256]{2,1,0:T(8,128)(2,1)S(1)}, u32[]{:S(2)}, u32[]{:S(2)}) collective-permute-start(bf16[8,456,256]{2,1,0:T(8,128)(2,1)S(1)} %get-tuple-element.153), channel_id=1, source_target_pairs={{0,16},{1,17},{2,18},{3,19},{4,20},{5,21},{6,22},{7,23},{8,9},{9,8... | collective-permute-start | bytes 5603336 | tf_op jit(solution)/shard_map/ppermute | solution.py:239
  49.8 31.2 %collective-permute-start.21 = (bf16[4,384,128]{2,1,0:T(8,128)(2,1)S(1)}, bf16[4,384,128]{2,1,0:T(8,128)(2,1)S(1)}, u32[]{:S(2)}, u32[]{:S(2)}) collective-permute-start(bf16[4,384,128]{2,1,0:T(8,128)(2,1)S(1)} %pad_maximum_fusion.3), channel_id=1, source_target_pairs={{0,1},{1,0},{2,3},{3,2},{4,5},{5,4},{6,7},{7,6},{8,24},{9,25},{10,... | collective-permute-start | bytes 1179656 | tf_op jit(solution)/shard_map/ppermute | solution.py:239
  55.7 15.6 %collective-permute-start.9 = (bf16[4,24,2304]{2,1,0:T(8,128)(2,1)S(1)}, bf16[4,24,2304]{2,1,0:T(8,128)(2,1)S(1)}, u32[]{:S(2)}, u32[]{:S(2)}) collective-permute-start(bf16[4,24,2304]{2,1,0:T(8,128)(2,1)S(1)} %pad_maximum_fusion.2), channel_id=1, source_target_pairs={{0,1},{1,0},{2,3},{3,2},{4,5},{5,4},{6,7},{7,6},{8,24},{9,25},{10,... | collective-permute-start | bytes 1327112 | tf_op jit(solution)/shard_map/ppermute | solution.py:239
  72.4 14.1 %collective-permute-start.10 = (bf16[8,24,2304]{2,1,0:T(8,128)(2,1)S(1)}, bf16[8,24,2304]{2,1,0:T(8,128)(2,1)S(1)}, u32[]{:S(2)}, u32[]{:S(2)}) collective-permute-start(bf16[8,24,2304]{2,1,0:T(8,128)(2,1)S(1)} %get-tuple-element.169), channel_id=1, source_target_pairs={{0,16},{1,17},{2,18},{3,19},{4,20},{5,21},{6,22},{7,23},{8,9},{9,8... | collective-permute-start | bytes 2654216 | tf_op jit(solution)/shard_map/ppermute | solution.py:239
  79.0 75.0 %collective-permute-start.17 = (bf16[16,456,256]{2,1,0:T(8,128)(2,1)}, bf16[16,456,256]{2,1,0:T(8,128)(2,1)}, u32[]{:S(2)}, u32[]{:S(2)}) collective-permute-start(bf16[16,456,256]{2,1,0:T(8,128)(2,1)} %get-tuple-element.149), channel_id=1, source_target_pairs={{0,8},{1,9},{2,10},{3,11},{4,12},{5,13},{6,14},{7,15},{8,0},{9,1},... | collective-permute-start | bytes 11206664 | tf_op jit(solution)/shard_map/ppermute | solution.py:239
  81.9 12.9 %collective-permute-start.22 = (bf16[8,384,128]{2,1,0:T(8,128)(2,1)S(1)}, bf16[8,384,128]{2,1,0:T(8,128)(2,1)S(1)}, u32[]{:S(2)}, u32[]{:S(2)}) collective-permute-start(bf16[8,384,128]{2,1,0:T(8,128)(2,1)S(1)} %get-tuple-element.174), channel_id=1, source_target_pairs={{0,16},{1,17},{2,18},{3,19},{4,20},{5,21},{6,22},{7,23},{8,9},{9,8... | collective-permute-start | bytes 2359304 | tf_op jit(solution)/shard_map/ppermute | solution.py:239
  86.4 9.6 %copy-start.13 = (bf16[72,3]{0,1:T(4,128)(2,1)S(1)}, bf16[72,3]{0,1:T(4,128)(2,1)}, u32[]{:S(2)}) copy-start(bf16[72,3]{0,1:T(4,128)(2,1)} %param.25) | copy-start | bytes 1300
  86.4 9.7 %copy-start.14 = (bf16[24]{0:T(256)(128)(2,1)S(1)}, bf16[24]{0:T(256)(128)(2,1)}, u32[]{:S(2)}) copy-start(bf16[24]{0:T(256)(128)(2,1)} %param.26) | copy-start | bytes 148
  86.4 10.0 %copy-start.15 = (bf16[24]{0:T(256)(128)(2,1)S(1)}, bf16[24]{0:T(256)(128)(2,1)}, u32[]{:S(2)}) copy-start(bf16[24]{0:T(256)(128)(2,1)} %param.27) | copy-start | bytes 148
  87.7 40.0 %collective-permute-start.11 = (bf16[16,24,2304]{2,1,0:T(8,128)(2,1)}, bf16[16,24,2304]{2,1,0:T(8,128)(2,1)}, u32[]{:S(2)}, u32[]{:S(2)}) collective-permute-start(bf16[16,24,2304]{2,1,0:T(8,128)(2,1)} %get-tuple-element.154), channel_id=1, source_target_pairs={{0,8},{1,9},{2,10},{3,11},{4,12},{5,13},{6,14},{7,15},{8,0},{9,1},... | collective-permute-start | bytes 5308424 | tf_op jit(solution)/shard_map/ppermute | solution.py:239
  96.0 30.0 %collective-permute-start.23 = (bf16[16,384,128]{2,1,0:T(8,128)(2,1)}, bf16[16,384,128]{2,1,0:T(8,128)(2,1)}, u32[]{:S(2)}, u32[]{:S(2)}) collective-permute-start(bf16[16,384,128]{2,1,0:T(8,128)(2,1)} %get-tuple-element.159), channel_id=1, source_target_pairs={{0,8},{1,9},{2,10},{3,11},{4,12},{5,13},{6,14},{7,15},{8,0},{9,1},... | collective-permute-start | bytes 4718600 | tf_op jit(solution)/shard_map/ppermute | solution.py:239
  96.6 9.6 %collective-permute-start = (bf16[1,8,128]{2,0,1:T(2,128)(2,1)S(1)}, bf16[1,8,128]{2,0,1:T(2,128)(2,1)S(1)}, u32[]{:S(2)}, u32[]{:S(2)}) collective-permute-start(bf16[1,8,128]{2,0,1:T(2,128)(2,1)S(1)} %scatter.20), channel_id=1, source_target_pairs={{0,2},{1,3},{2,0},{3,1},{4,6},{5,7},{6,4},{7,5},{8,10},{9,11},{10,... | collective-permute-start | bytes 6152 | tf_op jit(solution)/shard_map/ppermute | solution.py:239
  104.6 4.5 %collective-permute-start.1 = (bf16[1,8,128]{2,0,1:T(2,128)(2,1)S(1)}, bf16[1,8,128]{2,0,1:T(2,128)(2,1)S(1)}, u32[]{:S(2)}, u32[]{:S(2)}) collective-permute-start(bf16[1,8,128]{2,0,1:T(2,128)(2,1)S(1)} %scatter.20), channel_id=1, source_target_pairs={{0,4},{1,5},{2,6},{3,7},{4,0},{5,1},{6,2},{7,3},{8,12},{9,13},{10,... | collective-permute-start | bytes 6152 | tf_op jit(solution)/shard_map/ppermute | solution.py:239
  106.2 5.4 %collective-permute-start.2 = (bf16[1,8,128]{2,0,1:T(2,128)(2,1)S(1)}, bf16[1,8,128]{2,0,1:T(2,128)(2,1)S(1)}, u32[]{:S(2)}, u32[]{:S(2)}) collective-permute-start(bf16[1,8,128]{2,0,1:T(2,128)(2,1)S(1)} %scatter.20), channel_id=1, source_target_pairs={{0,6},{1,7},{2,4},{3,5},{4,2},{5,3},{6,0},{7,1},{8,14},{9,15},{10,... | collective-permute-start | bytes 6152 | tf_op jit(solution)/shard_map/ppermute | solution.py:239
  111.6 3.7 %collective-permute-start.3 = (bf16[4,8,128]{2,0,1:T(4,128)(2,1)S(1)}, bf16[4,8,128]{2,0,1:T(4,128)(2,1)S(1)}, u32[]{:S(2)}, u32[]{:S(2)}) collective-permute-start(bf16[4,8,128]{2,0,1:T(4,128)(2,1)S(1)} %pad_maximum_fusion.7), channel_id=1, source_target_pairs={{0,1},{1,0},{2,3},{3,2},{4,5},{5,4},{6,7},{7,6},{8,24},{9,25},{10,... | collective-permute-start | bytes 24584 | tf_op jit(solution)/shard_map/ppermute | solution.py:239
  115.4 3.8 %collective-permute-start.4 = (bf16[8,8,128]{2,0,1:T(8,128)(2,1)S(1)}, bf16[8,8,128]{2,0,1:T(8,128)(2,1)S(1)}, u32[]{:S(2)}, u32[]{:S(2)}) collective-permute-start(bf16[8,8,128]{2,0,1:T(8,128)(2,1)S(1)} %concatenate.96), channel_id=1, source_target_pairs={{0,16},{1,17},{2,18},{3,19},{4,20},{5,21},{6,22},{7,23},{8,9},{9,8... | collective-permute-start | bytes 49160 | tf_op jit(solution)/shard_map/ppermute | solution.py:239
  119.3 3.8 %collective-permute-start.5 = (bf16[16,8,128]{2,0,1:T(8,128)(2,1)S(1)}, bf16[16,8,128]{2,0,1:T(8,128)(2,1)S(1)}, u32[]{:S(2)}, u32[]{:S(2)}) collective-permute-start(bf16[16,8,128]{2,0,1:T(8,128)(2,1)S(1)} %concatenate.97), channel_id=1, source_target_pairs={{0,8},{1,9},{2,10},{3,11},{4,12},{5,13},{6,14},{7,15},{8,0},{9,1},... | collective-permute-start | bytes 98312 | tf_op jit(solution)/shard_map/ppermute | solution.py:239
  127.7 15.3 %copy-start.2 = (bf16[32,384,128]{2,1,0:T(8,128)(2,1)}, bf16[32,384,128]{2,1,0:T(8,128)(2,1)S(1)}, u32[]{:S(2)}) copy-start(bf16[32,384,128]{2,1,0:T(8,128)(2,1)S(1)} %constant_dynamic-update-slice_fusion.52.refs_0_.refs_1_.refs_2_.refs_3_.refs_4_.refs_5_.refs_6_.refs_7_) | copy-start | bytes 9437188
  217.8 9.5 %copy-start.11 = (f32[1,768]{1,0:T(1,128)S(1)}, f32[1,768]{1,0:T(1,128)}, u32[]{:S(2)}) copy-start(f32[1,768]{1,0:T(1,128)} %get-tuple-element.140) | copy-start | bytes 9220
  217.8 9.6 %copy-start.10 = (f32[8,768]{1,0:T(8,128)S(1)}, f32[8,768]{1,0:T(8,128)}, u32[]{:S(2)}) copy-start(f32[8,768]{1,0:T(8,128)} %get-tuple-element.136) | copy-start | bytes 73732
  217.8 9.6 %copy-start.9 = (f32[8,768]{1,0:T(8,128)S(1)}, f32[8,768]{1,0:T(8,128)}, u32[]{:S(2)}) copy-start(f32[8,768]{1,0:T(8,128)} %get-tuple-element.137) | copy-start | bytes 73732
  217.9 9.6 %copy-start.8 = (f32[8,768]{1,0:T(8,128)S(1)}, f32[8,768]{1,0:T(8,128)}, u32[]{:S(2)}) copy-start(f32[8,768]{1,0:T(8,128)} %get-tuple-element.138) | copy-start | bytes 73732
  227.7 7.7 %copy-start.7 = (s32[64]{0:T(128)S(1)}, s32[64]{0:T(128)}, u32[]{:S(2)}) copy-start(s32[64]{0:T(128)} %compare_select_fusion.1.meta) | copy-start | bytes 772
  227.7 16.4 %copy-start.16 = (bf16[16,384,128]{2,1,0:T(8,128)(2,1)S(1)}, bf16[16,384,128]{2,1,0:T(8,128)(2,1)}, u32[]{:S(2)}) copy-start(bf16[16,384,128]{2,1,0:T(8,128)(2,1)} %get-tuple-element.133) | copy-start | bytes 4718596
  234.4 20.9 %collective-permute-start.24 = (bf16[16,24,2304]{2,1,0:T(8,128)(2,1)}, bf16[16,24,2304]{2,1,0:T(8,128)(2,1)S(1)}, u32[]{:S(2)}, u32[]{:S(2)}) collective-permute-start(bf16[16,24,2304]{2,1,0:T(8,128)(2,1)} %bitcast.144), channel_id=1, source_target_pairs={{0,8},{1,9},{2,10},{3,11},{4,12},{5,13},{6,14},{7,15},{8,0},{9,1},... | collective-permute-start | bytes 5308424 | tf_op jit(solution)/shard_map/ppermute | solution.py:239
  235.6 2.9 collective-permute-start.37
  238.5 4.0 %collective-permute-start.38 = (f32[8,8,128]{2,1,0:T(8,128)S(1)}, f32[8,8,128]{2,1,0:T(8,128)S(1)}, u32[]{:S(2)}, u32[]{:S(2)}) collective-permute-start(f32[8,8,128]{2,1,0:T(8,128)S(1)} %slice.411), channel_id=1, source_target_pairs={{0,16},{1,17},{2,18},{3,19},{4,20},{5,21},{6,22},{7,23},{8,9},{9,8... | collective-permute-start | bytes 98312 | tf_op jit(solution)/shard_map/ppermute | solution.py:239
  242.5 3.8 %collective-permute-start.39 = (f32[4,8,128]{2,1,0:T(8,128)S(1)}, f32[4,8,128]{2,1,0:T(8,128)S(1)}, u32[]{:S(2)}, u32[]{:S(2)}) collective-permute-start(f32[4,8,128]{2,1,0:T(8,128)S(1)} %slice.413), channel_id=1, source_target_pairs={{0,1},{1,0},{2,3},{3,2},{4,5},{5,4},{6,7},{7,6},{8,24},{9,25},{10,... | collective-permute-start | bytes 49160 | tf_op jit(solution)/shard_map/ppermute | solution.py:239
  244.0 15.0 %collective-permute-start.30 = (bf16[16,384,128]{2,1,0:T(8,128)(2,1)S(1)}, bf16[16,384,128]{2,1,0:T(8,128)(2,1)S(1)}, u32[]{:S(2)}, u32[]{:S(2)}) collective-permute-start(bf16[16,384,128]{2,1,0:T(8,128)(2,1)S(1)} %copy-done.16), channel_id=1, source_target_pairs={{0,8},{1,9},{2,10},{3,11},{4,12},{5,13},{6,14},{7,15},{8,0},{9,1},... | collective-permute-start | bytes 4718600 | tf_op jit(solution)/shard_map/ppermute | solution.py:239
  246.3 4.4 %collective-permute-start.40 = (f32[8,128]{1,0:T(8,128)S(1)}, f32[8,128]{1,0:T(8,128)S(1)}, u32[]{:S(2)}, u32[]{:S(2)}) collective-permute-start(f32[8,128]{1,0:T(8,128)S(1)} %get-tuple-element.217), channel_id=1, source_target_pairs={{0,2},{1,3},{2,0},{3,1},{4,6},{5,7},{6,4},{7,5},{8,10},{9,11},{10,... | collective-permute-start | bytes 12296 | tf_op jit(solution)/shard_map/ppermute | solution.py:239
  246.6 4.8 %collective-permute-start.41 = (f32[8,128]{1,0:T(8,128)S(1)}, f32[8,128]{1,0:T(8,128)S(1)}, u32[]{:S(2)}, u32[]{:S(2)}) collective-permute-start(f32[8,128]{1,0:T(8,128)S(1)} %get-tuple-element.219), channel_id=1, source_target_pairs={{0,4},{1,5},{2,6},{3,7},{4,0},{5,1},{6,2},{7,3},{8,12},{9,13},{10,... | collective-permute-start | bytes 12296 | tf_op jit(solution)/shard_map/ppermute | solution.py:239
  249.9 5.4 %collective-permute-start.42 = (f32[8,128]{1,0:T(8,128)S(1)}, f32[8,128]{1,0:T(8,128)S(1)}, u32[]{:S(2)}, u32[]{:S(2)}) collective-permute-start(f32[8,128]{1,0:T(8,128)S(1)} %get-tuple-element.218), channel_id=1, source_target_pairs={{0,6},{1,7},{2,4},{3,5},{4,2},{5,3},{6,0},{7,1},{8,14},{9,15},{10,... | collective-permute-start | bytes 12296 | tf_op jit(solution)/shard_map/ppermute | solution.py:239
  250.8 46.2 %collective-permute-start.43 = (bf16[16,384,256]{2,1,0:T(8,128)(2,1)}, bf16[16,384,256]{2,1,0:T(8,128)(2,1)S(1)}, u32[]{:S(2)}, u32[]{:S(2)}) collective-permute-start(bf16[16,384,256]{2,1,0:T(8,128)(2,1)} %get-tuple-element.142), channel_id=1, source_target_pairs={{0,8},{1,9},{2,10},{3,11},{4,12},{5,13},{6,14},{7,15},{8,0},{9,1},... | collective-permute-start | bytes 9437192 | tf_op jit(solution)/shard_map/ppermute | solution.py:239
  251.5 7.4 %collective-permute-start.31 = (bf16[16,144,128]{2,1,0:T(8,128)(2,1)}, bf16[16,144,128]{2,1,0:T(8,128)(2,1)S(1)}, u32[]{:S(2)}, u32[]{:S(2)}) collective-permute-start(bf16[16,144,128]{2,1,0:T(8,128)(2,1)} %get-tuple-element.135), channel_id=1, source_target_pairs={{0,8},{1,9},{2,10},{3,11},{4,12},{5,13},{6,14},{7,15},{8,0},{9,1},... | collective-permute-start | bytes 1769480 | tf_op jit(solution)/shard_map/ppermute | solution.py:239
  255.3 3.6 %copy-start.5 = (bf16[16,144,128]{2,1,0:T(8,128)(2,1)S(1)}, bf16[16,144,128]{2,1,0:T(8,128)(2,1)}, u32[]{:S(2)}) copy-start(bf16[16,144,128]{2,1,0:T(8,128)(2,1)} %get-tuple-element.134) | copy-start | bytes 1769476
  257.3 14.4 %collective-permute-start.25 = (bf16[8,24,2304]{2,1,0:T(8,128)(2,1)S(1)}, bf16[8,24,2304]{2,1,0:T(8,128)(2,1)S(1)}, u32[]{:S(2)}, u32[]{:S(2)}) collective-permute-start(bf16[8,24,2304]{2,1,0:T(8,128)(2,1)S(1)} %slice.505), channel_id=1, source_target_pairs={{0,16},{1,17},{2,18},{3,19},{4,20},{5,21},{6,22},{7,23},{8,9},{9,8... | collective-permute-start | bytes 2654216 | tf_op jit(solution)/shard_map/ppermute | solution.py:239
  259.6 30.9 %collective-permute-start.32 = (bf16[8,528,128]{2,1,0:T(8,128)(2,1)S(1)}, bf16[8,528,128]{2,1,0:T(8,128)(2,1)S(1)}, u32[]{:S(2)}, u32[]{:S(2)}) collective-permute-start(bf16[8,528,128]{2,1,0:T(8,128)(2,1)S(1)} %fusion.2), channel_id=1, source_target_pairs={{0,16},{1,17},{2,18},{3,19},{4,20},{5,21},{6,22},{7,23},{8,9},{9,8... | collective-permute-start | bytes 3244040 | tf_op jit(solution)/shard_map/ppermute | solution.py:239
  271.9 20.5 %collective-permute-start.26 = (bf16[4,24,2304]{2,1,0:T(8,128)(2,1)S(1)}, bf16[4,24,2304]{2,1,0:T(8,128)(2,1)S(1)}, u32[]{:S(2)}, u32[]{:S(2)}) collective-permute-start(bf16[4,24,2304]{2,1,0:T(8,128)(2,1)S(1)} %slice.508), channel_id=1, source_target_pairs={{0,1},{1,0},{2,3},{3,2},{4,5},{5,4},{6,7},{7,6},{8,24},{9,25},{10,... | collective-permute-start | bytes 1327112 | tf_op jit(solution)/shard_map/ppermute | solution.py:239
  290.7 6.2 %copy-start.3 = (bf16[16,384,256]{2,1,0:T(8,128)(2,1)S(1)}, bf16[16,384,256]{2,1,0:T(8,128)(2,1)}, u32[]{:S(2)}) copy-start(bf16[16,384,256]{2,1,0:T(8,128)(2,1)} %get-tuple-element.141) | copy-start | bytes 9437188
  290.8 15.2 %collective-permute-start.33 = (bf16[4,528,128]{2,1,0:T(8,128)(2,1)S(1)}, bf16[4,528,128]{2,1,0:T(8,128)(2,1)S(1)}, u32[]{:S(2)}, u32[]{:S(2)}) collective-permute-start(bf16[4,528,128]{2,1,0:T(8,128)(2,1)S(1)} %slice.507), channel_id=1, source_target_pairs={{0,1},{1,0},{2,3},{3,2},{4,5},{5,4},{6,7},{7,6},{8,24},{9,25},{10,... | collective-permute-start | bytes 1622024 | tf_op jit(solution)/shard_map/ppermute | solution.py:239
  292.5 13.8 %collective-permute-start.27 = (bf16[24,2304]{1,0:T(8,128)(2,1)S(1)}, bf16[24,2304]{1,0:T(8,128)(2,1)S(1)}, u32[]{:S(2)}, u32[]{:S(2)}) collective-permute-start(bf16[24,2304]{1,0:T(8,128)(2,1)S(1)} %get-tuple-element.164), channel_id=1, source_target_pairs={{0,2},{1,3},{2,0},{3,1},{4,6},{5,7},{6,4},{7,5},{8,10},{9,11},{10,... | collective-permute-start | bytes 331784 | tf_op jit(solution)/shard_map/ppermute | solution.py:239
  292.6 13.8 %collective-permute-start.28 = (bf16[24,2304]{1,0:T(8,128)(2,1)S(1)}, bf16[24,2304]{1,0:T(8,128)(2,1)S(1)}, u32[]{:S(2)}, u32[]{:S(2)}) collective-permute-start(bf16[24,2304]{1,0:T(8,128)(2,1)S(1)} %get-tuple-element.166), channel_id=1, source_target_pairs={{0,4},{1,5},{2,6},{3,7},{4,0},{5,1},{6,2},{7,3},{8,12},{9,13},{10,... | collective-permute-start | bytes 331784 | tf_op jit(solution)/shard_map/ppermute | solution.py:239
  292.6 18.0 %collective-permute-start.29 = (bf16[24,2304]{1,0:T(8,128)(2,1)S(1)}, bf16[24,2304]{1,0:T(8,128)(2,1)S(1)}, u32[]{:S(2)}, u32[]{:S(2)}) collective-permute-start(bf16[24,2304]{1,0:T(8,128)(2,1)S(1)} %get-tuple-element.165), channel_id=1, source_target_pairs={{0,6},{1,7},{2,4},{3,5},{4,2},{5,3},{6,0},{7,1},{8,14},{9,15},{10,... | collective-permute-start | bytes 331784 | tf_op jit(solution)/shard_map/ppermute | solution.py:239
  298.0 21.2 %collective-permute-start.44 = (bf16[8,384,256]{2,1,0:T(8,128)(2,1)S(1)}, bf16[8,384,256]{2,1,0:T(8,128)(2,1)S(1)}, u32[]{:S(2)}, u32[]{:S(2)}) collective-permute-start(bf16[8,384,256]{2,1,0:T(8,128)(2,1)S(1)} %slice.504), channel_id=1, source_target_pairs={{0,16},{1,17},{2,18},{3,19},{4,20},{5,21},{6,22},{7,23},{8,9},{9,8... | collective-permute-start | bytes 4718600 | tf_op jit(solution)/shard_map/ppermute | solution.py:239
  306.2 6.5 %collective-permute-start.34 = (bf16[528,128]{1,0:T(8,128)(2,1)S(1)}, bf16[528,128]{1,0:T(8,128)(2,1)S(1)}, u32[]{:S(2)}, u32[]{:S(2)}) collective-permute-start(bf16[528,128]{1,0:T(8,128)(2,1)S(1)} %get-tuple-element.161), channel_id=1, source_target_pairs={{0,2},{1,3},{2,0},{3,1},{4,6},{5,7},{6,4},{7,5},{8,10},{9,11},{10,... | collective-permute-start | bytes 405512 | tf_op jit(solution)/shard_map/ppermute | solution.py:239
  306.3 8.9 %collective-permute-start.35 = (bf16[528,128]{1,0:T(8,128)(2,1)S(1)}, bf16[528,128]{1,0:T(8,128)(2,1)S(1)}, u32[]{:S(2)}, u32[]{:S(2)}) collective-permute-start(bf16[528,128]{1,0:T(8,128)(2,1)S(1)} %get-tuple-element.163), channel_id=1, source_target_pairs={{0,4},{1,5},{2,6},{3,7},{4,0},{5,1},{6,2},{7,3},{8,12},{9,13},{10,... | collective-permute-start | bytes 405512 | tf_op jit(solution)/shard_map/ppermute | solution.py:239
  306.4 8.8 %collective-permute-start.36 = (bf16[528,128]{1,0:T(8,128)(2,1)S(1)}, bf16[528,128]{1,0:T(8,128)(2,1)S(1)}, u32[]{:S(2)}, u32[]{:S(2)}) collective-permute-start(bf16[528,128]{1,0:T(8,128)(2,1)S(1)} %get-tuple-element.162), channel_id=1, source_target_pairs={{0,6},{1,7},{2,4},{3,5},{4,2},{5,3},{6,0},{7,1},{8,14},{9,15},{10,... | collective-permute-start | bytes 405512 | tf_op jit(solution)/shard_map/ppermute | solution.py:239
  319.6 12.1 %collective-permute-start.45 = (bf16[4,384,256]{2,1,0:T(8,128)(2,1)S(1)}, bf16[4,384,256]{2,1,0:T(8,128)(2,1)S(1)}, u32[]{:S(2)}, u32[]{:S(2)}) collective-permute-start(bf16[4,384,256]{2,1,0:T(8,128)(2,1)S(1)} %slice.506), channel_id=1, source_target_pairs={{0,1},{1,0},{2,3},{3,2},{4,5},{5,4},{6,7},{7,6},{8,24},{9,25},{10,... | collective-permute-start | bytes 2359304 | tf_op jit(solution)/shard_map/ppermute | solution.py:239
  331.7 15.0 %copy-start.1 = (bf16[384,768]{1,0:T(8,128)(2,1)S(1)}, bf16[384,768]{1,0:T(8,128)(2,1)}, u32[]{:S(2)}) copy-start(bf16[384,768]{1,0:T(8,128)(2,1)} %param.29) | copy-start | bytes 1769476
  332.0 7.9 %collective-permute-start.46 = (bf16[384,256]{1,0:T(8,128)(2,1)S(1)}, bf16[384,256]{1,0:T(8,128)(2,1)S(1)}, u32[]{:S(2)}, u32[]{:S(2)}) collective-permute-start(bf16[384,256]{1,0:T(8,128)(2,1)S(1)} %get-tuple-element.156), channel_id=1, source_target_pairs={{0,2},{1,3},{2,0},{3,1},{4,6},{5,7},{6,4},{7,5},{8,10},{9,11},{10,... | collective-permute-start | bytes 589832 | tf_op jit(solution)/shard_map/ppermute | solution.py:239
  333.1 12.6 %collective-permute-start.47 = (bf16[384,256]{1,0:T(8,128)(2,1)S(1)}, bf16[384,256]{1,0:T(8,128)(2,1)S(1)}, u32[]{:S(2)}, u32[]{:S(2)}) collective-permute-start(bf16[384,256]{1,0:T(8,128)(2,1)S(1)} %get-tuple-element.158), channel_id=1, source_target_pairs={{0,4},{1,5},{2,6},{3,7},{4,0},{5,1},{6,2},{7,3},{8,12},{9,13},{10,... | collective-permute-start | bytes 589832 | tf_op jit(solution)/shard_map/ppermute | solution.py:239
  333.1 12.6 %collective-permute-start.48 = (bf16[384,256]{1,0:T(8,128)(2,1)S(1)}, bf16[384,256]{1,0:T(8,128)(2,1)S(1)}, u32[]{:S(2)}, u32[]{:S(2)}) collective-permute-start(bf16[384,256]{1,0:T(8,128)(2,1)S(1)} %get-tuple-element.157), channel_id=1, source_target_pairs={{0,6},{1,7},{2,4},{3,5},{4,2},{5,3},{6,0},{7,1},{8,14},{9,15},{10,... | collective-permute-start | bytes 589832 | tf_op jit(solution)/shard_map/ppermute | solution.py:239
  336.4 10.3 %copy-start.12 = (f32[24,768]{1,0:T(8,128)}, f32[24,768]{1,0:T(8,128)S(1)}, u32[]{:S(2)}) copy-start(f32[24,768]{1,0:T(8,128)S(1)} %constant_dynamic-update-slice_fusion.59) | copy-start | bytes 221188
  (2 other events, 2.9 us)
